TPU v7x, 256 devices: a whole 4x4x8 slice. The times are simulated.
256 devices in a mesh: gx: 16 (over x, y), gy: 16 (over z, core).
Axes of the slice: x: 4, y: 4, z: 8, core: 2. Of those that a mesh axis runs over, the one named last changes fastest.
Arguments:
- permeability: float32 [1, 16, 128, 2048], P(None, None, 'gx', 'gy'), may hold values from 0.2 to 5
- saturation: float32 [1, 16, 128, 2048], P(None, None, 'gx', 'gy'), may hold values from 0.1 to 0.9
- pressure_old: float32 [1, 16, 128, 2048], P(None, None, 'gx', 'gy'), may hold values from -6 to 6
- source: float32 [16, 128, 2048], P(None, 'gx', 'gy'), may hold values from -25 to 25
Outputs:
- pressure: float32 [1, 16, 128, 2048], P(None, None, 'gx', 'gy')
- saturation_new: float32 [1, 16, 128, 2048], P(None, None, 'gx', 'gy')
All inputs are finite; a program needn't handle non-finite values.
Results may differ from a plain program's by a relative error of at most 0.0003.
Values sent between devices are 32-bit elements; how exact they have to be, the bound alone decides.
No kernel may reach another device: no remote copies, remote signals or barrier semaphores. Data moves between devices by JAX's collectives and lax.ppermute only.
A program may use at most 64 MiB of HBM per device.

v0:
```python
import jax
import jax.numpy as jnp
from jax import lax
from jax.sharding import PartitionSpec as P

ITERS = 2


storage_term = 0.5
vertical_ratio = 0.1
step_ratio = 0.05
water_viscosity = 1.0
oil_viscosity = 2.0


def padded_2(x, sides, width):
    for axis, dim in sides:
        size, length = (lax.axis_size(axis), x.shape[dim])
        up = [(i, (i + 1) % size) for i in range(size - 1)]
        down = [(j, i) for i, j in up]
        last = lax.slice_in_dim(x, length - width, length, axis=dim)
        first = lax.slice_in_dim(x, 0, width, axis=dim)
        before = lax.ppermute(last, axis, up)
        after = lax.ppermute(first, axis, down)
        x = jnp.concatenate([before, x, after], axis=dim)
    return x


def total_mobility(values):
    return values * values / water_viscosity + (1.0 - values) * (1.0 - values) / oil_viscosity


def water_fraction(values):
    return values * values / water_viscosity / total_mobility(values)


def coefficient(perm_left, perm_right, mobile_left, mobile_right, scaling):
    summed = perm_left + perm_right
    guarded = jnp.where(summed > 0.0, summed, 1.0)
    harmonic = jnp.where(summed > 0.0, 2.0 * perm_left * perm_right / guarded, 0.0)
    return scaling * harmonic * (0.5 * (mobile_left + mobile_right))


def across_pairs(padded, border, margin):
    rows_across = padded.shape[-2] - 2 * border
    rows_along = padded.shape[-1] - 2 * border
    block = padded[
        ...,
        border - margin - 1 : border + rows_across + margin + 1,
        border - margin : border + rows_along + margin,
    ]
    return (block[..., :-1, :], block[..., 1:, :])


def along_pairs(padded, border, margin):
    rows_across = padded.shape[-2] - 2 * border
    rows_along = padded.shape[-1] - 2 * border
    block = padded[
        ...,
        border - margin : border + rows_across + margin,
        border - margin - 1 : border + rows_along + margin + 1,
    ]
    return (block[..., :-1], block[..., 1:])


def interior(padded, border, margin):
    rows_across = padded.shape[-2] - 2 * border
    rows_along = padded.shape[-1] - 2 * border
    return padded[
        ...,
        border - margin : border + rows_across + margin,
        border - margin : border + rows_along + margin,
    ]


def vertical_pairs(values):
    widened = jnp.pad(values, ((0, 0), (1, 1), (0, 0), (0, 0)))
    return (widened[:, :-1], widened[:, 1:])


def face_terms(perm_wide, sat_wide, border, margin):
    mobile = total_mobility(sat_wide)
    perm_left, perm_right = across_pairs(perm_wide, border, margin)
    mobile_left, mobile_right = across_pairs(mobile, border, margin)
    across = coefficient(perm_left, perm_right, mobile_left, mobile_right, 1.0)
    perm_left, perm_right = along_pairs(perm_wide, border, margin)
    mobile_left, mobile_right = along_pairs(mobile, border, margin)
    along = coefficient(perm_left, perm_right, mobile_left, mobile_right, 1.0)
    perm_low, perm_high = vertical_pairs(interior(perm_wide, border, margin))
    mobile_low, mobile_high = vertical_pairs(interior(mobile, border, margin))
    vertical = coefficient(perm_low, perm_high, mobile_low, mobile_high, vertical_ratio)
    return (across, along, vertical)


def divergence(terms):
    across, along, vertical = terms
    return (
        vertical[:, 1:]
        - vertical[:, :-1]
        + (across[..., 1:, :] - across[..., :-1, :])
        + (along[..., 1:] - along[..., :-1])
    )


def diagonal_of(terms):
    across, along, vertical = terms
    return (
        storage_term
        + (vertical[:, 1:] + vertical[:, :-1])
        + (across[..., 1:, :] + across[..., :-1, :])
        + (along[..., 1:] + along[..., :-1])
    )


def fluxes(terms, pressure_wide, border, margin):
    across, along, vertical = terms
    left_side, right_side = across_pairs(pressure_wide, border, margin)
    flow_across = across * (left_side - right_side)
    left_side, right_side = along_pairs(pressure_wide, border, margin)
    flow_along = along * (left_side - right_side)
    lower_side, upper_side = vertical_pairs(interior(pressure_wide, border, margin))
    flow_vertical = vertical * (lower_side - upper_side)
    return (flow_across, flow_along, flow_vertical)


def apply_operator(terms, padded):
    return storage_term * interior(padded, 1, 0) + divergence(fluxes(terms, padded, 1, 0))


def transport(flows, sat_wide, border, margin, inflow_rate):
    fraction = water_fraction(sat_wide)
    flow_across, flow_along, flow_vertical = flows
    left_side, right_side = across_pairs(fraction, border, margin)
    water_across = flow_across * jnp.where(flow_across > 0.0, left_side, right_side)
    left_side, right_side = along_pairs(fraction, border, margin)
    water_along = flow_along * jnp.where(flow_along > 0.0, left_side, right_side)
    middle = interior(fraction, border, margin)
    lower_side, upper_side = vertical_pairs(middle)
    water_vertical = flow_vertical * jnp.where(flow_vertical > 0.0, lower_side, upper_side)
    current = interior(sat_wide, border, margin)
    gained = jnp.maximum(inflow_rate, 0.0) + jnp.minimum(inflow_rate, 0.0) * middle
    return current + step_ratio * (gained - divergence((water_across, water_along, water_vertical)))


def search_image(terms, values):
    padded = padded_2(values, (("gx", 2), ("gy", 3)), 1)
    return (apply_operator(terms, padded), padded)


def local_dot(former, latter):
    return jnp.sum(former * latter, axis=(1, 2, 3))


def per_sample(scalars):
    return scalars[:, None, None, None]


def energy(residual, precond):
    return lax.psum(local_dot(residual, precond), ("gx", "gy"))


def local(permeability, saturation, pressure_old, source):
    samples = permeability.shape[0]
    inflow_rate = source[None]
    stacked = jnp.concatenate([permeability, saturation, pressure_old], axis=0)
    padded = padded_2(stacked, (("gx", 2), ("gy", 3)), 1)
    border = 1
    perm_wide = padded[:samples]
    sat_wide = padded[samples : 2 * samples]
    old_wide = padded[2 * samples : 3 * samples]
    wide_terms = face_terms(perm_wide, sat_wide, border, border - 1)
    diagonal = diagonal_of(wide_terms)
    right_side = inflow_rate + storage_term * pressure_old
    solution = pressure_old
    residual = right_side - apply_operator(wide_terms, old_wide)
    precond = residual / diagonal
    direction = precond
    energy_now = energy(residual, precond)
    for sweep in range(ITERS):
        image_field, direction_wide = search_image(wide_terms, direction)
        curvature = lax.psum(local_dot(direction, image_field), ("gx", "gy"))
        step_size = energy_now / curvature
        solution = solution + per_sample(step_size) * direction
        if sweep + 1 < ITERS:
            residual = residual - per_sample(step_size) * image_field
            precond = residual / diagonal
            energy_next = energy(residual, precond)
            direction = precond + per_sample(energy_next / energy_now) * direction
            energy_now = energy_next
    pressure_wide = padded_2(solution, (("gx", 2), ("gy", 3)), 1)
    flows = fluxes(wide_terms, pressure_wide, 1, 0)
    first = transport(flows, sat_wide, 1, 0, inflow_rate)
    first_wide = padded_2(first, (("gx", 2), ("gy", 3)), 1)
    second = transport(flows, first_wide, 1, 0, inflow_rate)
    return (solution, second)


def solution(mesh):
    in_specs = (
        P(None, None, "gx", "gy"),
        P(None, None, "gx", "gy"),
        P(None, None, "gx", "gy"),
        P(None, "gx", "gy"),
    )
    out_specs = (P(None, None, "gx", "gy"), P(None, None, "gx", "gy"))
    return jax.shard_map(local, mesh=mesh, in_specs=in_specs, out_specs=out_specs, check_vma=False)
```

profile of v0, /device:TPU:1, one launch (start us, length us, event | category | flops | bytes accessed | tf_op | source)
XLA Modules:
  0.0 340.0 jit_solution(17763078292054774674)
XLA Ops:
  2.4 4.0 %collective-permute-start = (f32[3,16,1,128]{3,2,1,0:T(1,128)S(1)}, f32[3,16,1,128]{3,2,1,0:T(1,128)S(1)}, u32[]{:S(2)}, u32[]{:S(2)}) collective-permute-start(f32[3,16,1,128]{3,2,1,0:T(1,128)S(1)} %get-tuple-element.22), channel_id=1, source_target_pairs={{0,16},{16,32},{32,48},{48,64},{64,80},{80,96},{96,112},{112,128},... | collective-permute-start | bytes 73736 | tf_op jit(solution)/shard_map/ppermute | solution.py:23
  6.4 1.3 collective-permute-start.1
  7.7 3.3 collective-permute-done.1
  11.3 5.5 %collective-permute-start.2 = (f32[3,16,10,1]{3,2,1,0:T(8,128)S(1)}, f32[3,16,10,1]{3,2,1,0:T(8,128)S(1)}, u32[]{:S(2)}, u32[]{:S(2)}) collective-permute-start(f32[3,16,10,1]{3,2,1,0:T(8,128)S(1)} %get-tuple-element.20), channel_id=1, source_target_pairs={{0,1},{1,2},{2,3},{3,4},{4,5},{5,6},{6,7},{7,8},{8,9},{9,10},{10,1... | collective-permute-start | bytes 5768 | tf_op jit(solution)/shard_map/ppermute | solution.py:23
  16.8 1.9 collective-permute-start.3
  18.7 2.8 collective-permute-done.2
  21.5 4.4 %collective-permute-done.3 = f32[3,16,10,1]{3,2,1,0:T(8,128)S(1)} collective-permute-done((f32[3,16,10,1]{3,2,1,0:T(8,128)S(1)}, f32[3,16,10,1]{3,2,1,0:T(8,128)S(1)}, u32[]{:S(2)}, u32[]{:S(2)}) %collective-permute-start.3) | collective-permute-done | bytes 1952 | tf_op jit(solution)/shard_map/ppermute | solution.py:24
  28.3 3.2 collective-permute-start.4
  31.5 1.3 collective-permute-start.5
  33.0 3.0 collective-permute-done.5
  36.1 3.2 collective-permute-start.6
  39.2 1.9 collective-permute-start.7
  41.2 4.3 %collective-permute-done.7 = f32[1,16,10,1]{3,2,1,0:T(8,128)S(1)} collective-permute-done((f32[1,16,10,1]{3,2,1,0:T(8,128)S(1)}, f32[1,16,10,1]{3,2,1,0:T(8,128)S(1)}, u32[]{:S(2)}, u32[]{:S(2)}) %collective-permute-start.7) | collective-permute-done | bytes 672 | tf_op jit(solution)/shard_map/ppermute | solution.py:24
  46.4 83.0 %all-reduce.8 = (f32[1]{0:T(128)}, f32[1]{0:T(128)}) all-reduce(f32[1]{0:T(128)} %bitcast.1, f32[1]{0:T(128)} %bitcast.2), channel_id=1, replica_groups=mesh['gx'=16,'gy'=16] {'gx','gy'}, use_global_device_ids=true, to_apply=%region_1.2 | all-reduce | flops 2 | bytes 16 | tf_op jit(solution)/shard_map/psum | solution.py:159
  131.4 72.6 %psum.30 = f32[1]{0:T(128)} all-reduce(f32[1]{0:T(128)} %bitcast.4), channel_id=1, replica_groups=mesh['gx'=16,'gy'=16] {'gx','gy'}, use_global_device_ids=true, to_apply=%region_5.6 | all-reduce | flops 1 | bytes 8 | tf_op jit(solution)/shard_map/psum | solution.py:159
  205.4 3.0 collective-permute-start.8
  208.4 1.3 collective-permute-start.9
  209.7 3.1 collective-permute-done.9
  212.9 5.5 %collective-permute-start.10 = (f32[1,16,10,1]{3,2,1,0:T(8,128)S(1)}, f32[1,16,10,1]{3,2,1,0:T(8,128)S(1)}, u32[]{:S(2)}, u32[]{:S(2)}) collective-permute-start(f32[1,16,10,1]{3,2,1,0:T(8,128)S(1)} %get-tuple-element.28), channel_id=1, source_target_pairs={{0,1},{1,2},{2,3},{3,4},{4,5},{5,6},{6,7},{7,8},{8,9},{9,10},{10,1... | collective-permute-start | bytes 1928 | tf_op jit(solution)/shard_map/ppermute | solution.py:23
  218.5 1.9 collective-permute-start.11
  220.5 4.3 %collective-permute-done.11 = f32[1,16,10,1]{3,2,1,0:T(8,128)S(1)} collective-permute-done((f32[1,16,10,1]{3,2,1,0:T(8,128)S(1)}, f32[1,16,10,1]{3,2,1,0:T(8,128)S(1)}, u32[]{:S(2)}, u32[]{:S(2)}) %collective-permute-start.11) | collective-permute-done | bytes 672 | tf_op jit(solution)/shard_map/ppermute | solution.py:24
  225.6 76.7 %psum.31 = f32[1]{0:T(128)} all-reduce(f32[1]{0:T(128)} %bitcast.6), channel_id=1, replica_groups=mesh['gx'=16,'gy'=16] {'gx','gy'}, use_global_device_ids=true, to_apply=%region_7.8 | all-reduce | flops 1 | bytes 8 | tf_op jit(solution)/shard_map/psum | solution.py:181
  303.7 3.1 collective-permute-start.12
  308.1 3.1 collective-permute-done.13
  311.3 4.4 %collective-permute-start.14 = (f32[1,16,10,1]{3,2,1,0:T(8,128)S(1)}, f32[1,16,10,1]{3,2,1,0:T(8,128)S(1)}, u32[]{:S(2)}, u32[]{:S(2)}) collective-permute-start(f32[1,16,10,1]{3,2,1,0:T(8,128)S(1)} %get-tuple-element.26), channel_id=1, source_target_pairs={{0,1},{1,2},{2,3},{3,4},{4,5},{5,6},{6,7},{7,8},{8,9},{9,10},{10,1... | collective-permute-start | bytes 1928 | tf_op jit(solution)/shard_map/ppermute | solution.py:23
  315.7 1.9 collective-permute-start.15
  317.8 4.2 %collective-permute-done.15 = f32[1,16,10,1]{3,2,1,0:T(8,128)S(1)} collective-permute-done((f32[1,16,10,1]{3,2,1,0:T(8,128)S(1)}, f32[1,16,10,1]{3,2,1,0:T(8,128)S(1)}, u32[]{:S(2)}, u32[]{:S(2)}) %collective-permute-start.15) | collective-permute-done | bytes 672 | tf_op jit(solution)/shard_map/ppermute | solution.py:24
  322.3 2.3 collective-permute-start.16
  325.9 3.4 collective-permute-done.17
  329.4 2.9 collective-permute-start.18
  332.3 1.9 collective-permute-start.19
  334.2 4.3 %collective-permute-done.19 = f32[1,16,10,1]{3,2,1,0:T(8,128)S(1)} collective-permute-done((f32[1,16,10,1]{3,2,1,0:T(8,128)S(1)}, f32[1,16,10,1]{3,2,1,0:T(8,128)S(1)}, u32[]{:S(2)}, u32[]{:S(2)}) %collective-permute-start.19) | collective-permute-done | bytes 672 | tf_op jit(solution)/shard_map/ppermute | solution.py:24
  (68 shorter events, 11.8 us)
Async XLA Ops:
  0.6 0.9 copy-start.3
  1.5 0.8 copy-start.1
  2.4 5.3 %collective-permute-start = (f32[3,16,1,128]{3,2,1,0:T(1,128)S(1)}, f32[3,16,1,128]{3,2,1,0:T(1,128)S(1)}, u32[]{:S(2)}, u32[]{:S(2)}) collective-permute-start(f32[3,16,1,128]{3,2,1,0:T(1,128)S(1)} %get-tuple-element.22), channel_id=1, source_target_pairs={{0,16},{16,32},{32,48},{48,64},{64,80},{80,96},{96,112},{112,128},... | collective-permute-start | bytes 73736 | tf_op jit(solution)/shard_map/ppermute | solution.py:23
  6.4 4.6 %collective-permute-start.1 = (f32[3,16,1,128]{3,2,1,0:T(1,128)S(1)}, f32[3,16,1,128]{3,2,1,0:T(1,128)S(1)}, u32[]{:S(2)}, u32[]{:S(2)}) collective-permute-start(f32[3,16,1,128]{3,2,1,0:T(1,128)S(1)} %get-tuple-element.23), channel_id=1, source_target_pairs={{16,0},{32,16},{48,32},{64,48},{80,64},{96,80},{112,96},{128,112},... | collective-permute-start | bytes 73736 | tf_op jit(solution)/shard_map/ppermute | solution.py:24
  11.3 10.2 %collective-permute-start.2 = (f32[3,16,10,1]{3,2,1,0:T(8,128)S(1)}, f32[3,16,10,1]{3,2,1,0:T(8,128)S(1)}, u32[]{:S(2)}, u32[]{:S(2)}) collective-permute-start(f32[3,16,10,1]{3,2,1,0:T(8,128)S(1)} %get-tuple-element.20), channel_id=1, source_target_pairs={{0,1},{1,2},{2,3},{3,4},{4,5},{5,6},{6,7},{7,8},{8,9},{9,10},{10,1... | collective-permute-start | bytes 5768 | tf_op jit(solution)/shard_map/ppermute | solution.py:23
  16.8 9.1 %collective-permute-start.3 = (f32[3,16,10,1]{3,2,1,0:T(8,128)S(1)}, f32[3,16,10,1]{3,2,1,0:T(8,128)S(1)}, u32[]{:S(2)}, u32[]{:S(2)}) collective-permute-start(f32[3,16,10,1]{3,2,1,0:T(8,128)S(1)} %get-tuple-element.21), channel_id=1, source_target_pairs={{1,0},{2,1},{3,2},{4,3},{5,4},{6,5},{7,6},{8,7},{9,8},{10,9},{11,1... | collective-permute-start | bytes 5768 | tf_op jit(solution)/shard_map/ppermute | solution.py:24
  26.2 0.8 copy-start.4
  27.3 0.8 copy-start.2
  28.3 4.6 %collective-permute-start.4 = (f32[1,16,1,128]{3,2,1,0:T(1,128)S(1)}, f32[1,16,1,128]{3,2,1,0:T(1,128)S(1)}, u32[]{:S(2)}, u32[]{:S(2)}) collective-permute-start(f32[1,16,1,128]{3,2,1,0:T(1,128)S(1)} %get-tuple-element.38), channel_id=1, source_target_pairs={{0,16},{16,32},{32,48},{48,64},{64,80},{80,96},{96,112},{112,128},... | collective-permute-start | bytes 24584 | tf_op jit(solution)/shard_map/ppermute | solution.py:23
  31.5 4.4 %collective-permute-start.5 = (f32[1,16,1,128]{3,2,1,0:T(1,128)S(1)}, f32[1,16,1,128]{3,2,1,0:T(1,128)S(1)}, u32[]{:S(2)}, u32[]{:S(2)}) collective-permute-start(f32[1,16,1,128]{3,2,1,0:T(1,128)S(1)} %get-tuple-element.39), channel_id=1, source_target_pairs={{16,0},{32,16},{48,32},{64,48},{80,64},{96,80},{112,96},{128,112},... | collective-permute-start | bytes 24584 | tf_op jit(solution)/shard_map/ppermute | solution.py:24
  36.1 5.2 %collective-permute-start.6 = (f32[1,16,10,1]{3,2,1,0:T(8,128)S(1)}, f32[1,16,10,1]{3,2,1,0:T(8,128)S(1)}, u32[]{:S(2)}, u32[]{:S(2)}) collective-permute-start(f32[1,16,10,1]{3,2,1,0:T(8,128)S(1)} %get-tuple-element.30), channel_id=1, source_target_pairs={{0,1},{1,2},{2,3},{3,4},{4,5},{5,6},{6,7},{7,8},{8,9},{9,10},{10,1... | collective-permute-start | bytes 1928 | tf_op jit(solution)/shard_map/ppermute | solution.py:23
  39.2 6.3 %collective-permute-start.7 = (f32[1,16,10,1]{3,2,1,0:T(8,128)S(1)}, f32[1,16,10,1]{3,2,1,0:T(8,128)S(1)}, u32[]{:S(2)}, u32[]{:S(2)}) collective-permute-start(f32[1,16,10,1]{3,2,1,0:T(8,128)S(1)} %get-tuple-element.31), channel_id=1, source_target_pairs={{1,0},{2,1},{3,2},{4,3},{5,4},{6,5},{7,6},{8,7},{9,8},{10,9},{11,1... | collective-permute-start | bytes 1928 | tf_op jit(solution)/shard_map/ppermute | solution.py:24
  205.4 4.3 %collective-permute-start.8 = (f32[1,16,1,128]{3,2,1,0:T(1,128)S(1)}, f32[1,16,1,128]{3,2,1,0:T(1,128)S(1)}, u32[]{:S(2)}, u32[]{:S(2)}) collective-permute-start(f32[1,16,1,128]{3,2,1,0:T(1,128)S(1)} %get-tuple-element.36), channel_id=1, source_target_pairs={{0,16},{16,32},{32,48},{48,64},{64,80},{80,96},{96,112},{112,128},... | collective-permute-start | bytes 24584 | tf_op jit(solution)/shard_map/ppermute | solution.py:23
  208.4 4.4 %collective-permute-start.9 = (f32[1,16,1,128]{3,2,1,0:T(1,128)S(1)}, f32[1,16,1,128]{3,2,1,0:T(1,128)S(1)}, u32[]{:S(2)}, u32[]{:S(2)}) collective-permute-start(f32[1,16,1,128]{3,2,1,0:T(1,128)S(1)} %get-tuple-element.37), channel_id=1, source_target_pairs={{16,0},{32,16},{48,32},{64,48},{80,64},{96,80},{112,96},{128,112},... | collective-permute-start | bytes 24584 | tf_op jit(solution)/shard_map/ppermute | solution.py:24
  212.9 7.5 %collective-permute-start.10 = (f32[1,16,10,1]{3,2,1,0:T(8,128)S(1)}, f32[1,16,10,1]{3,2,1,0:T(8,128)S(1)}, u32[]{:S(2)}, u32[]{:S(2)}) collective-permute-start(f32[1,16,10,1]{3,2,1,0:T(8,128)S(1)} %get-tuple-element.28), channel_id=1, source_target_pairs={{0,1},{1,2},{2,3},{3,4},{4,5},{5,6},{6,7},{7,8},{8,9},{9,10},{10,1... | collective-permute-start | bytes 1928 | tf_op jit(solution)/shard_map/ppermute | solution.py:23
  218.5 6.3 %collective-permute-start.11 = (f32[1,16,10,1]{3,2,1,0:T(8,128)S(1)}, f32[1,16,10,1]{3,2,1,0:T(8,128)S(1)}, u32[]{:S(2)}, u32[]{:S(2)}) collective-permute-start(f32[1,16,10,1]{3,2,1,0:T(8,128)S(1)} %get-tuple-element.29), channel_id=1, source_target_pairs={{1,0},{2,1},{3,2},{4,3},{5,4},{6,5},{7,6},{8,7},{9,8},{10,9},{11,1... | collective-permute-start | bytes 1928 | tf_op jit(solution)/shard_map/ppermute | solution.py:24
  303.6 35.4 %copy-start = (f32[1,16,8,128]{3,2,1,0:T(8,128)}, f32[1,16,8,128]{3,2,1,0:T(8,128)S(1)}, u32[]{:S(2)}) copy-start(f32[1,16,8,128]{3,2,1,0:T(8,128)S(1)} %multiply_add_fusion.1) | copy-start | bytes 196612
  303.7 4.4 %collective-permute-start.12 = (f32[1,16,1,128]{3,2,1,0:T(1,128)S(1)}, f32[1,16,1,128]{3,2,1,0:T(1,128)S(1)}, u32[]{:S(2)}, u32[]{:S(2)}) collective-permute-start(f32[1,16,1,128]{3,2,1,0:T(1,128)S(1)} %get-tuple-element.34), channel_id=1, source_target_pairs={{0,16},{16,32},{32,48},{48,64},{64,80},{80,96},{96,112},{112,128},... | collective-permute-start | bytes 24584 | tf_op jit(solution)/shard_map/ppermute | solution.py:23
  306.8 4.4 %collective-permute-start.13 = (f32[1,16,1,128]{3,2,1,0:T(1,128)S(1)}, f32[1,16,1,128]{3,2,1,0:T(1,128)S(1)}, u32[]{:S(2)}, u32[]{:S(2)}) collective-permute-start(f32[1,16,1,128]{3,2,1,0:T(1,128)S(1)} %get-tuple-element.35), channel_id=1, source_target_pairs={{16,0},{32,16},{48,32},{64,48},{80,64},{96,80},{112,96},{128,112},... | collective-permute-start | bytes 24584 | tf_op jit(solution)/shard_map/ppermute | solution.py:24
  311.3 6.4 %collective-permute-start.14 = (f32[1,16,10,1]{3,2,1,0:T(8,128)S(1)}, f32[1,16,10,1]{3,2,1,0:T(8,128)S(1)}, u32[]{:S(2)}, u32[]{:S(2)}) collective-permute-start(f32[1,16,10,1]{3,2,1,0:T(8,128)S(1)} %get-tuple-element.26), channel_id=1, source_target_pairs={{0,1},{1,2},{2,3},{3,4},{4,5},{5,6},{6,7},{7,8},{8,9},{9,10},{10,1... | collective-permute-start | bytes 1928 | tf_op jit(solution)/shard_map/ppermute | solution.py:23
  315.7 6.3 %collective-permute-start.15 = (f32[1,16,10,1]{3,2,1,0:T(8,128)S(1)}, f32[1,16,10,1]{3,2,1,0:T(8,128)S(1)}, u32[]{:S(2)}, u32[]{:S(2)}) collective-permute-start(f32[1,16,10,1]{3,2,1,0:T(8,128)S(1)} %get-tuple-element.27), channel_id=1, source_target_pairs={{1,0},{2,1},{3,2},{4,3},{5,4},{6,5},{7,6},{8,7},{9,8},{10,9},{11,1... | collective-permute-start | bytes 1928 | tf_op jit(solution)/shard_map/ppermute | solution.py:24
  322.3 3.6 %collective-permute-start.16 = (f32[1,16,1,128]{3,2,1,0:T(1,128)S(1)}, f32[1,16,1,128]{3,2,1,0:T(1,128)S(1)}, u32[]{:S(2)}, u32[]{:S(2)}) collective-permute-start(f32[1,16,1,128]{3,2,1,0:T(1,128)S(1)} %get-tuple-element.32), channel_id=1, source_target_pairs={{0,16},{16,32},{32,48},{48,64},{64,80},{80,96},{96,112},{112,128},... | collective-permute-start | bytes 24584 | tf_op jit(solution)/shard_map/ppermute | solution.py:23
  324.6 4.7 %collective-permute-start.17 = (f32[1,16,1,128]{3,2,1,0:T(1,128)S(1)}, f32[1,16,1,128]{3,2,1,0:T(1,128)S(1)}, u32[]{:S(2)}, u32[]{:S(2)}) collective-permute-start(f32[1,16,1,128]{3,2,1,0:T(1,128)S(1)} %get-tuple-element.33), channel_id=1, source_target_pairs={{16,0},{32,16},{48,32},{64,48},{80,64},{96,80},{112,96},{128,112},... | collective-permute-start | bytes 24584 | tf_op jit(solution)/shard_map/ppermute | solution.py:24
  329.4 4.9 %collective-permute-start.18 = (f32[1,16,10,1]{3,2,1,0:T(8,128)S(1)}, f32[1,16,10,1]{3,2,1,0:T(8,128)S(1)}, u32[]{:S(2)}, u32[]{:S(2)}) collective-permute-start(f32[1,16,10,1]{3,2,1,0:T(8,128)S(1)} %get-tuple-element.24), channel_id=1, source_target_pairs={{0,1},{1,2},{2,3},{3,4},{4,5},{5,6},{6,7},{7,8},{8,9},{9,10},{10,1... | collective-permute-start | bytes 1928 | tf_op jit(solution)/shard_map/ppermute | solution.py:23
  332.3 6.3 %collective-permute-start.19 = (f32[1,16,10,1]{3,2,1,0:T(8,128)S(1)}, f32[1,16,10,1]{3,2,1,0:T(8,128)S(1)}, u32[]{:S(2)}, u32[]{:S(2)}) collective-permute-start(f32[1,16,10,1]{3,2,1,0:T(8,128)S(1)} %get-tuple-element.25), channel_id=1, source_target_pairs={{1,0},{2,1},{3,2},{4,3},{5,4},{6,5},{7,6},{8,7},{9,8},{10,9},{11,1... | collective-permute-start | bytes 1928 | tf_op jit(solution)/shard_map/ppermute | solution.py:24
where the time goes:
time: 345 us; the launch traced here: 340 us
  blocking collectives  232 us (67%)
  starting transfers between devices  53.2 us (15%)
  waiting for transfers between devices  40.1 us (12%)
  other arithmetic  5.19 us (2%)
  between operations  5.09 us (1%)
  local copies, waits for them, and re-layouts  4.04 us (1%)
    psum x2, blocking collectives, energy(): return lax.psum(local_dot(residual, precond), ('gx', 'gy'))  156 us
    psum x1, blocking collectives, local(): curvature = lax.psum(local_dot(direction, image_field), ('gx', 'gy'))  76.7 us
    ppermute x10, waiting for transfers between devices, padded_2(): after = lax.ppermute(first, axis, down)  37.3 us
    ppermute x10, starting transfers between devices, padded_2(): before = lax.ppermute(last, axis, up)  37.2 us
    ppermute x10, starting transfers between devices, padded_2(): after = lax.ppermute(first, axis, down)  16.1 us
  transfers between devices with their start and end apart: 20, of which 11 were waited for; matrix products, arithmetic and copies ran while one was open for 0% of the time, Pallas kernels for 0%

commit v1 on v0

v1 whole, which is shorter than its diff:
```python
import jax
import jax.numpy as jnp
from jax import lax
from jax.sharding import PartitionSpec as P

storage_term = 0.5
vertical_ratio = 0.1
step_ratio = 0.05
water_viscosity = 1.0
oil_viscosity = 2.0

HALO = 4


def padded(x, axis, dim, width):
    size, length = lax.axis_size(axis), x.shape[dim]
    up = [(i, i + 1) for i in range(size - 1)]
    down = [(i + 1, i) for i in range(size - 1)]
    last = lax.slice_in_dim(x, length - width, length, axis=dim)
    first = lax.slice_in_dim(x, 0, width, axis=dim)
    before = lax.ppermute(last, axis, up)
    after = lax.ppermute(first, axis, down)
    return jnp.concatenate([before, x, after], axis=dim)


def total_mobility(s):
    return s * s / water_viscosity + (1.0 - s) * (1.0 - s) / oil_viscosity


def pairs(x, dim):
    n = x.shape[dim]
    return lax.slice_in_dim(x, 0, n - 1, axis=dim), lax.slice_in_dim(x, 1, n, axis=dim)


def coefficient(perm, mobile, dim, scaling):
    ka, kb = pairs(perm, dim)
    ma, mb = pairs(mobile, dim)
    summed = ka + kb
    safe = jnp.where(summed > 0.0, summed, 1.0)
    return scaling * (2.0 * ka * kb / safe) * (0.5 * (ma + mb))


def both_sides(face, dim):
    widths = [(0, 0)] * face.ndim
    widths[dim] = (1, 1)
    return pairs(jnp.pad(face, widths), dim)


def divergence(faces):
    total = None
    for dim, face in enumerate(faces):
        lower, upper = both_sides(face, dim)
        change = upper - lower
        total = change if total is None else total + change
    return total


def fluxes(terms, v):
    out = []
    for dim, term in enumerate(terms):
        a, b = pairs(v, dim)
        out.append(term * (a - b))
    return out


def apply_operator(terms, v):
    return storage_term * v + divergence(fluxes(terms, v))


def transport(flows, s, rate):
    fraction = s * s / water_viscosity / total_mobility(s)
    water = []
    for dim, flow in enumerate(flows):
        a, b = pairs(fraction, dim)
        water.append(flow * jnp.where(flow > 0.0, a, b))
    gained = jnp.maximum(rate, 0.0) + jnp.minimum(rate, 0.0) * fraction
    return s + step_ratio * (gained - divergence(water))


def one_sample(permeability, saturation, pressure_old, source):
    stacked = jnp.stack([permeability, saturation, pressure_old, source])
    wide = padded(padded(stacked, "gx", 2, HALO), "gy", 3, HALO)
    perm, sat, old, rate = wide[0], wide[1], wide[2], wide[3]
    mobile = total_mobility(sat)
    terms = [coefficient(perm, mobile, dim, vertical_ratio if dim == 0 else 1.0) for dim in range(3)]
    diagonal = storage_term
    for dim, term in enumerate(terms):
        lower, upper = both_sides(term, dim)
        diagonal = diagonal + (upper + lower)
    residual = rate + storage_term * old - apply_operator(terms, old)
    first = residual / diagonal
    image = apply_operator(terms, first)
    second = (image - residual) / diagonal
    second_image = apply_operator(terms, second)
    own = lambda x: x[:, HALO:-HALO, HALO:-HALO]
    r, z, g, v, w = (own(x) for x in (residual, first, image, second, second_image))
    partial = jnp.stack([jnp.sum(t) for t in (r * z, z * g, z * (g - r), v * g, v * w)])
    size = lax.axis_size("gx") * lax.axis_size("gy")
    row = jnp.pad(partial, (0, 123))
    sums = lax.all_to_all(jnp.broadcast_to(row, (size, 128)), ("gx", "gy"), 0, 0, tiled=True).sum(0)
    rz, zaz, rv, vaz, vav = (sums[i] for i in range(5))
    ratio = vaz / zaz
    bottom = vav - ratio * vaz
    top = rv - ratio * rz
    b = jnp.where(bottom > 0.0, top / bottom, 0.0)
    a = rz / zaz - b * ratio
    new = old + a * first + b * second
    flows = fluxes(terms, new)
    s = transport(flows, sat, rate)
    s = transport(flows, s, rate)
    return own(new), own(s)


def local(permeability, saturation, pressure_old, source):
    outs = [one_sample(permeability[i], saturation[i], pressure_old[i], source) for i in range(permeability.shape[0])]
    return jnp.stack([o[0] for o in outs]), jnp.stack([o[1] for o in outs])


def solution(mesh):
    field = P(None, None, "gx", "gy")
    return jax.shard_map(local, mesh=mesh, in_specs=(field, field, field, P(None, "gx", "gy")), out_specs=(field, field), check_vma=False)
```

time: 345 us -> 72.3 us (0.21); the launches traced: 340 us -> 71.9 us
  blocking collectives: 232 us -> 28.1 us
  starting transfers between devices: 53.2 us -> 12.9 us
  waiting for transfers between devices: 40.1 us -> 13 us
    psum x3 -> x0, blocking collectives: 232 us -> none  [the longest x2 156 us: energy(): return lax.psum(local_dot(residual, precond), ('gx', 'gy'))]
    ppermute x20 -> x4, starting transfers between devices: 53.2 us -> 12.9 us  [the longest x2 9.69 us: padded(): before = lax.ppermute(last, axis, up)]
    all_to_all x0 -> x1, blocking collectives: none -> 28.1 us  [one_sample(): lax.all_to_all(jnp.broadcast_to(row, (size, 128)), ('gx', 'gy'), 0, 0, ti...]
    ppermute x20 -> x4, waiting for transfers between devices: 40.1 us -> 13 us  [the longest x2 7.95 us: padded(): after = lax.ppermute(first, axis, down)]
    another operation x0 -> x2, local copies, waits for them, and re-layouts: none -> 3.95 us  [the longest x1 3.24 us: one_sample(): jnp.stack([jnp.sum(t) for t in (r * z, z * g, z * (g - r), v * g, v * w)])]
  transfers between devices with their start and end apart: 20 -> 4, of which waited for: 11 -> 4; matrix products, arithmetic and copies ran while one was open for 0% -> 0% of each run, Pallas kernels for 0% -> 0%
where the time goes in v1:
time: 72.3 us; the launch traced here: 71.9 us
  blocking collectives  28.1 us (39%)
  waiting for transfers between devices  13 us (18%)
  starting transfers between devices  12.9 us (18%)
  other arithmetic  6.43 us (9%)
  between operations  6.03 us (8%)
  local copies, waits for them, and re-layouts  5.5 us (8%)
    all_to_all x1, blocking collectives, one_sample(): lax.all_to_all(jnp.broadcast_to(row, (size, 128)), ('gx', 'gy'), 0, 0, ti...  28.1 us
    ppermute x2, starting transfers between devices, padded(): before = lax.ppermute(last, axis, up)  9.69 us
    ppermute x2, waiting for transfers between devices, padded(): after = lax.ppermute(first, axis, down)  7.95 us
    ppermute x2, waiting for transfers between devices, padded(): before = lax.ppermute(last, axis, up)  5.03 us
    another operation x1, local copies, waits for them, and re-layouts, one_sample(): jnp.stack([jnp.sum(t) for t in (r * z, z * g, z * (g - r), v * g, v * w)])  3.24 us
    ppermute x2, starting transfers between devices, padded(): after = lax.ppermute(first, axis, down)  3.21 us
  transfers between devices with their start and end apart: 4, of which 4 were waited for; matrix products, arithmetic and copies ran while one was open for 0% of the time, Pallas kernels for 0%

profile of v1, /device:TPU:1, one launch (start us, length us, event | category | flops | bytes accessed | tf_op | source)
XLA Modules:
  0.0 71.9 jit_solution(13442360621692366910)
XLA Ops:
  0.6 1.0 %pad_maximum_fusion.2 = f32[4,16,8,128]{3,2,1,0:T(8,128)S(1)} fusion(f32[1,16,8,128]{3,2,1,0:T(8,128)} %bitcast.66, f32[1,16,8,128]{3,2,1,0:T(8,128)} %param.6, f32[1,16,8,128]{3,2,1,0:T(8,128)} %param.5, f32[1,16,8,128]{3,2,1,0:T(8,128)} %param.4), kind=kLoop, calls=%fused_computation.89 | loop fusion | flops 196608 | bytes 524288 | tf_op jit(solution)/shard_map/stack | solution.py:81
  1.7 4.2 %collective-permute-start = (f32[4,16,4,128]{3,2,1,0:T(4,128)S(1)}, f32[4,16,4,128]{3,2,1,0:T(4,128)S(1)}, u32[]{:S(2)}, u32[]{:S(2)}) collective-permute-start(f32[4,16,4,128]{3,2,1,0:T(4,128)S(1)} %get-tuple-element.39), channel_id=1, source_target_pairs={{0,16},{16,32},{32,48},{48,64},{64,80},{80,96},{96,112},{112,128},... | collective-permute-start | bytes 393224 | tf_op jit(solution)/shard_map/ppermute | solution.py:21
  5.9 1.3 %collective-permute-start.1 = (f32[4,16,4,128]{3,2,1,0:T(4,128)S(1)}, f32[4,16,4,128]{3,2,1,0:T(4,128)S(1)}, u32[]{:S(2)}, u32[]{:S(2)}) collective-permute-start(f32[4,16,4,128]{3,2,1,0:T(4,128)S(1)} %get-tuple-element.40), channel_id=1, source_target_pairs={{16,0},{32,16},{48,32},{64,48},{80,64},{96,80},{112,96},{128,112},... | collective-permute-start | bytes 393224 | tf_op jit(solution)/shard_map/ppermute | solution.py:22
  7.2 0.9 %collective-permute-done = f32[4,16,4,128]{3,2,1,0:T(4,128)S(1)} collective-permute-done((f32[4,16,4,128]{3,2,1,0:T(4,128)S(1)}, f32[4,16,4,128]{3,2,1,0:T(4,128)S(1)}, u32[]{:S(2)}, u32[]{:S(2)}) %collective-permute-start) | collective-permute-done | bytes 131104 | tf_op jit(solution)/shard_map/ppermute | solution.py:21
  8.0 3.6 %collective-permute-done.1 = f32[4,16,4,128]{3,2,1,0:T(4,128)S(1)} collective-permute-done((f32[4,16,4,128]{3,2,1,0:T(4,128)S(1)}, f32[4,16,4,128]{3,2,1,0:T(4,128)S(1)}, u32[]{:S(2)}, u32[]{:S(2)}) %collective-permute-start.1) | collective-permute-done | bytes 131104 | tf_op jit(solution)/shard_map/ppermute | solution.py:22
  11.6 0.1 pad_maximum_fusion.1
  11.7 0.2 fusion.72
  11.9 5.5 %collective-permute-start.2 = (f32[4,16,16,4]{3,2,1,0:T(8,128)S(1)}, f32[4,16,16,4]{3,2,1,0:T(8,128)S(1)}, u32[]{:S(2)}, u32[]{:S(2)}) collective-permute-start(f32[4,16,16,4]{3,2,1,0:T(8,128)S(1)} %get-tuple-element.29), channel_id=1, source_target_pairs={{0,1},{1,2},{2,3},{3,4},{4,5},{5,6},{6,7},{7,8},{8,9},{9,10},{10,1... | collective-permute-start | bytes 49160 | tf_op jit(solution)/shard_map/ppermute | solution.py:21
  17.4 1.9 %collective-permute-start.3 = (f32[4,16,16,4]{3,2,1,0:T(8,128)S(1)}, f32[4,16,16,4]{3,2,1,0:T(8,128)S(1)}, u32[]{:S(2)}, u32[]{:S(2)}) collective-permute-start(f32[4,16,16,4]{3,2,1,0:T(8,128)S(1)} %get-tuple-element.30), channel_id=1, source_target_pairs={{1,0},{2,1},{3,2},{4,3},{5,4},{6,5},{7,6},{8,7},{9,8},{10,9},{11,1... | collective-permute-start | bytes 49160 | tf_op jit(solution)/shard_map/ppermute | solution.py:22
  19.4 4.2 %collective-permute-done.2 = f32[4,16,16,4]{3,2,1,0:T(8,128)S(1)} collective-permute-done((f32[4,16,16,4]{3,2,1,0:T(8,128)S(1)}, f32[4,16,16,4]{3,2,1,0:T(8,128)S(1)}, u32[]{:S(2)}, u32[]{:S(2)}) %collective-permute-start.2) | collective-permute-done | bytes 16416 | tf_op jit(solution)/shard_map/ppermute | solution.py:21
  23.5 4.4 %collective-permute-done.3 = f32[4,16,16,4]{3,2,1,0:T(8,128)S(1)} collective-permute-done((f32[4,16,16,4]{3,2,1,0:T(8,128)S(1)}, f32[4,16,16,4]{3,2,1,0:T(8,128)S(1)}, u32[]{:S(2)}, u32[]{:S(2)}) %collective-permute-start.3) | collective-permute-done | bytes 16416 | tf_op jit(solution)/shard_map/ppermute | solution.py:22
  27.9 0.8 %pad_maximum_fusion = f32[4,16,16,136]{3,2,1,0:T(8,128)S(1)} fusion(f32[4,16,16,4]{3,2,1,0:T(8,128)S(1)} %collective-permute-done.3, f32[4,16,4,128]{3,2,1,0:T(4,128)S(1)} %collective-permute-done.1, f32[1,16,8,128]{3,2,1,0:T(8,128)S(1)} %bitcast.68, f32[1,16,8,128]{3,2,1,0:T(8,128)S(1)} %copy-done.1, f32[1,16,8,128]{3,2,1,0:T(8,128)S(1)} %copy-done.2, ...), kind=kLoop, calls=%fused_computation | loop fusion | flops 974848 | bytes 1114112 | tf_op jit(solution)/shard_map/concatenate | solution.py:23
  28.7 0.1 fusion.52
  28.9 0.2 fusion.39
  29.1 0.3 fusion.37
  29.4 0.1 fusion.50
  29.5 0.4 fusion.66
  29.9 0.1 fusion.35
  30.1 0.2 subtract_divide_fusion
  30.4 0.1 fusion.33
  30.5 0.1 pad_slice_fusion.27
  30.7 0.1 pad_slice_fusion.5
  30.8 0.9 %fusion.62 = (f32[]{:T(128)}, f32[]{:T(128)}, f32[]{:T(128)}, f32[]{:T(128)}, f32[]{:T(128)}) fusion(f32[16,16,136]{2,1,0:T(8,128)S(1)} %get-tuple-element.38, f32[16,16,136]{2,1,0:T(8,128)S(1)} %get-tuple-element.37, f32[16,16,136]{2,1,0:T(8,128)S(1)} %get-tuple-element.36, f32[16,16,136]{2,1,0:T(8,128)S(1)} %get-tuple-element.35, ...), kind=kLoop, calls=%fused_computation.139 | loop fusion | flops 294907 | bytes 655380 | tf_op jit(solution)/shard_map/reduce_sum | solution.py:97
  31.7 3.2 %stack.37 = f32[5]{0:T(128)S(1)} concatenate(f32[1]{0:T(128)} %bitcast.8, f32[1]{0:T(128)} %bitcast.9, f32[1]{0:T(128)} %bitcast.10, f32[1]{0:T(128)} %bitcast.11, f32[1]{0:T(128)} %bitcast.12), dimensions={0} | concatenate | bytes 40 | tf_op jit(solution)/shard_map/stack | solution.py:97
  35.0 28.1 %all_to_all.6 = f32[256,1,128]{2,1,0:T(1,128)S(1)} all-to-all(f32[256,1,128]{2,1,0:T(1,128)S(1)} %broadcast_in_dim.18), channel_id=1, replica_groups=mesh['gx'=16,'gy'=16] {'gx','gy'}, dimensions={0} | all-to-all | bytes 262144 | tf_op jit(solution)/shard_map/all_to_all | solution.py:100
  63.2 0.7 fusion.74
  69.2 0.2 fusion.29
  69.4 0.3 add_divide_fusion
  69.9 0.2 fusion.27
  70.1 0.7 slice_bitcast_fusion.6
  70.9 0.1 pad_slice_fusion.25
  71.0 0.9 %fusion.54 = f32[1,16,8,128]{3,2,1,0:T(8,128)} fusion(f32[16,16,136]{2,1,0:T(8,128)S(1)} %get-tuple-element.11, f32[16,16,136]{2,1,0:T(8,128)S(1)} %get-tuple-element.25, f32[16,16,136]{2,1,0:T(8,128)S(1)} %get-tuple-element.34, f32[16,16,136]{2,1,0:T(8,128)S(1)} %get-tuple-element.33, f32[16,16,136]{2,1,0:T(8,128)S(1)} %get-tuple-element.10, ...), kind=kLoop, calls=%fused_computation.124 | loop fusion | flops 163840 | bytes 720896 | tf_op jit(solution)/shard_map/stack | solution.py:116
  (24 shorter events, 0.9 us)
Async XLA Ops:
  1.6 10.0 %copy-start = (f32[16,8,128]{2,1,0:T(8,128)S(1)}, f32[16,8,128]{2,1,0:T(8,128)}, u32[]{:S(2)}) copy-start(f32[16,8,128]{2,1,0:T(8,128)} %param.7) | copy-start | bytes 196612
  1.6 10.0 %copy-start.1 = (f32[1,16,8,128]{3,2,1,0:T(8,128)S(1)}, f32[1,16,8,128]{3,2,1,0:T(8,128)}, u32[]{:S(2)}) copy-start(f32[1,16,8,128]{3,2,1,0:T(8,128)} %param.6) | copy-start | bytes 196612
  1.6 10.0 %copy-start.2 = (f32[1,16,8,128]{3,2,1,0:T(8,128)S(1)}, f32[1,16,8,128]{3,2,1,0:T(8,128)}, u32[]{:S(2)}) copy-start(f32[1,16,8,128]{3,2,1,0:T(8,128)} %param.5) | copy-start | bytes 196612
  1.6 10.0 %copy-start.3 = (f32[1,16,8,128]{3,2,1,0:T(8,128)S(1)}, f32[1,16,8,128]{3,2,1,0:T(8,128)}, u32[]{:S(2)}) copy-start(f32[1,16,8,128]{3,2,1,0:T(8,128)} %param.4) | copy-start | bytes 196612
  1.7 6.3 %collective-permute-start = (f32[4,16,4,128]{3,2,1,0:T(4,128)S(1)}, f32[4,16,4,128]{3,2,1,0:T(4,128)S(1)}, u32[]{:S(2)}, u32[]{:S(2)}) collective-permute-start(f32[4,16,4,128]{3,2,1,0:T(4,128)S(1)} %get-tuple-element.39), channel_id=1, source_target_pairs={{0,16},{16,32},{32,48},{48,64},{64,80},{80,96},{96,112},{112,128},... | collective-permute-start | bytes 393224 | tf_op jit(solution)/shard_map/ppermute | solution.py:21
  5.9 5.7 %collective-permute-start.1 = (f32[4,16,4,128]{3,2,1,0:T(4,128)S(1)}, f32[4,16,4,128]{3,2,1,0:T(4,128)S(1)}, u32[]{:S(2)}, u32[]{:S(2)}) collective-permute-start(f32[4,16,4,128]{3,2,1,0:T(4,128)S(1)} %get-tuple-element.40), channel_id=1, source_target_pairs={{16,0},{32,16},{48,32},{64,48},{80,64},{96,80},{112,96},{128,112},... | collective-permute-start | bytes 393224 | tf_op jit(solution)/shard_map/ppermute | solution.py:22
  11.9 11.6 %collective-permute-start.2 = (f32[4,16,16,4]{3,2,1,0:T(8,128)S(1)}, f32[4,16,16,4]{3,2,1,0:T(8,128)S(1)}, u32[]{:S(2)}, u32[]{:S(2)}) collective-permute-start(f32[4,16,16,4]{3,2,1,0:T(8,128)S(1)} %get-tuple-element.29), channel_id=1, source_target_pairs={{0,1},{1,2},{2,3},{3,4},{4,5},{5,6},{6,7},{7,8},{8,9},{9,10},{10,1... | collective-permute-start | bytes 49160 | tf_op jit(solution)/shard_map/ppermute | solution.py:21
  17.4 10.5 %collective-permute-start.3 = (f32[4,16,16,4]{3,2,1,0:T(8,128)S(1)}, f32[4,16,16,4]{3,2,1,0:T(8,128)S(1)}, u32[]{:S(2)}, u32[]{:S(2)}) collective-permute-start(f32[4,16,16,4]{3,2,1,0:T(8,128)S(1)} %get-tuple-element.30), channel_id=1, source_target_pairs={{1,0},{2,1},{3,2},{4,3},{5,4},{6,5},{7,6},{8,7},{9,8},{10,9},{11,1... | collective-permute-start | bytes 49160 | tf_op jit(solution)/shard_map/ppermute | solution.py:22

commit v2 on v1

v2 whole, which is shorter than its diff:
```python
import jax
import jax.numpy as jnp
from jax import lax
from jax.experimental import pallas as pl
from jax.experimental.pallas import tpu as pltpu
from jax.sharding import PartitionSpec as P

storage_term = 0.5
vertical_ratio = 0.1
step_ratio = 0.05
water_viscosity = 1.0
oil_viscosity = 2.0

NZ, ROWS, LANES, HALO = 16, 8, 128, 4
SPAN = 2 * ROWS
SEG = 16
TILES = NZ * SEG // LANES
PER = LANES // SEG
F32 = jnp.float32


def lanes(shape=(ROWS, LANES)):
    return lax.broadcasted_iota(jnp.int32, shape, len(shape) - 1)


def sublanes(shape=(ROWS, LANES)):
    return lax.broadcasted_iota(jnp.int32, shape, len(shape) - 2)


def turn(x, by, axis):
    n = x.shape[axis]
    if isinstance(by, int):
        by %= n
        if by == 0:
            return x
    return pltpu.roll(x, by, axis)


def total_mobility(s):
    return s * s / water_viscosity + (1.0 - s) * (1.0 - s) / oil_viscosity


def water_fraction(s):
    return s * s / water_viscosity / total_mobility(s)


def coefficient(ka, kb, ma, mb):
    return ka * kb * (ma + mb) / jnp.maximum(ka + kb, 1e-30)


def row_next(x):
    return turn(x, -1, 0)


def row_prev(x):
    return turn(x, 1, 0)


def col_next(x):
    return turn(x, -1, 1)


def col_prev(x):
    return turn(x, 1, 1)


def pack_columns(k, s, p, q, to_prev, to_next):
    seg = lanes() % SEG // 4
    layer = lanes() // SEG
    for t in range(TILES):
        first = jnp.zeros((ROWS, LANES), F32)
        last = jnp.zeros((ROWS, LANES), F32)
        for zz in range(PER):
            for i, ref in enumerate((k, s, p, q)):
                x = ref[t * PER + zz]
                here = (layer == zz) & (seg == i)
                at = zz * SEG + 4 * i
                first = jnp.where(here, turn(x, at, 1), first)
                last = jnp.where(here, turn(x, at + HALO, 1), last)
        to_prev[t] = first
        to_next[t] = last


def pack_rows(k, s, p, q, own_first, own_last, from_prev, from_next, packed, to_prev, to_next):
    seg = lanes() % SEG // 4
    low = sublanes() < HALO

    def pair(at, a, b):
        to_prev[at] = jnp.where(low, a, turn(b, HALO, 0))
        to_next[at] = jnp.where(low, turn(a, HALO, 0), b)

    for t in range(TILES):
        cols = []
        for i in range(4):
            x = turn(from_prev[t], -4 * i, 1)
            x = jnp.where(seg == 1, turn(own_first[t], 4 - 4 * i, 1), x)
            x = jnp.where(seg == 2, turn(own_last[t], 8 - 4 * i, 1), x)
            x = jnp.where(seg == 3, turn(from_next[t], 12 - 4 * i, 1), x)
            packed[i, t] = x
            cols.append(x)
        pair(2 * NZ + t, cols[0], cols[1])
        pair(2 * NZ + TILES + t, cols[2], cols[3])

    for z in range(NZ):
        pair(z, k[z], s[z])
        pair(NZ + z, p[z], q[z])


def layer_next(x):
    edge = lanes((SPAN, LANES)) < LANES - SEG
    moved = [turn(t, -SEG, 1) for t in x]
    return [jnp.where(edge, moved[i], moved[(i + 1) % TILES]) for i in range(TILES)]


def layer_prev(x):
    edge = lanes((SPAN, LANES)) >= SEG
    moved = [turn(t, SEG, 1) for t in x]
    return [jnp.where(edge, moved[i], moved[(i - 1) % TILES]) for i in range(TILES)]


def each(f, *args):
    return [f(*a) for a in zip(*args)]


def packed_divergence(flows):
    fx, fy, fz = flows
    return each(lambda x, xp, y, yp, z, zp: (z - zp) + (x - xp) + (y - yp), fx, each(row_prev, fx), fy, each(col_prev, fy), fz, layer_prev(fz))


def packed_flows(terms, v):
    nexts = (each(row_next, v), each(col_next, v), layer_next(v))
    return [each(lambda c, a, b: c * (a - b), term, v, n) for term, n in zip(terms, nexts)]


def edge_next(y, packed_face, z):
    at = LANES - 1 - (z % PER * SEG + 11)
    return jnp.where(lanes((SPAN, LANES)) == LANES - 1, pltpu.roll(packed_face[z // PER], at, 1), y)


def edge_prev(y, packed_face, z):
    at = LANES - (z % PER * SEG + 3)
    return jnp.where(lanes((SPAN, LANES)) == 0, pltpu.roll(packed_face[z // PER], at, 1), col_prev(y))


def middle(k_own, s_own, p_own, q_own, packed, prev, nxt,
           sums, z0, v, s, q, fp, fz, fv, s_pack, q_pack, fp_pack, fz_pack, fv_pack,
           k, p, cx, cy, cz, inv, r, cy_pack):
    gx, gy = lax.axis_index("gx"), lax.axis_index("gy")
    last_gx, last_gy = lax.axis_size("gx") - 1, lax.axis_size("gy") - 1
    row8 = sublanes()
    low = row8 < HALO
    inside_rows = jnp.where(low, jnp.where(gx == last_gx, 0.0, 1.0), jnp.where(gx == 0, 0.0, 1.0))
    seg8 = lanes() % SEG // 4
    inside_cols = jnp.where(seg8 == 0, jnp.where(gy == 0, 0.0, 1.0), jnp.where(seg8 == 3, jnp.where(gy == last_gy, 0.0, 1.0), 1.0))

    def halo_rows(at):
        below, above = nxt[at], prev[at]
        return jnp.where(low, below, turn(above, HALO, 0)), jnp.where(low, turn(below, HALO, 0), above)

    def assemble(z, _):
        ka, sa = halo_rows(z)
        pa, qa = halo_rows(NZ + z)
        k[z, :ROWS], k[z, ROWS:] = k_own[z], ka * inside_rows
        s[z, :ROWS], s[z, ROWS:] = s_own[z], sa
        p[z, :ROWS], p[z, ROWS:] = p_own[z], pa
        q[z, :ROWS], q[z, ROWS:] = q_own[z], qa
        return _

    lax.fori_loop(0, NZ, assemble, 0)

    kp, sp, pp, qp = [], [], [], []
    for t in range(TILES):
        ka, sa = halo_rows(2 * NZ + t)
        pa, qa = halo_rows(2 * NZ + TILES + t)
        kp.append(jnp.concatenate([packed[0, t] * inside_cols, ka * inside_rows * inside_cols], 0))
        sp.append(jnp.concatenate([packed[1, t], sa], 0))
        pp.append(jnp.concatenate([packed[2, t], pa], 0))
        qp.append(jnp.concatenate([packed[3, t], qa], 0))
    mp = each(total_mobility, sp)
    tx = each(coefficient, kp, each(row_next, kp), mp, each(row_next, mp))
    ty = each(coefficient, kp, each(col_next, kp), mp, each(col_next, mp))
    tz = each(coefficient, kp, layer_next(kp), mp, layer_next(mp))
    tz = each(lambda c: vertical_ratio * c, tz)
    tz[-1] = jnp.where(lanes((SPAN, LANES)) < LANES - SEG, tz[-1], 0.0)
    terms = (tx, ty, tz)
    diag = each(lambda x, xp, y, yp, z, zp: storage_term + (z + zp) + (x + xp) + (y + yp), tx, each(row_prev, tx), ty, each(col_prev, ty), tz, layer_prev(tz))
    ip = each(lambda d: 1.0 / d, diag)
    flows_p = packed_flows(terms, pp)
    rp = each(lambda a, d: a - d, qp, packed_divergence(flows_p))
    zp0 = each(lambda a, b: a * b, rp, ip)
    flows_z = packed_flows(terms, zp0)
    gp = each(lambda a, d: storage_term * a + d, zp0, packed_divergence(flows_z))
    vp = each(lambda a, b, c: (a - b) * c, gp, rp, ip)
    flows_v = packed_flows(terms, vp)
    for t in range(TILES):
        s_pack[t], q_pack[t], cy_pack[t] = sp[t], qp[t], ty[t]
        for d in range(3):
            fp_pack[d, t], fz_pack[d, t], fv_pack[d, t] = flows_p[d][t], flows_z[d][t], flows_v[d][t]

    def first(z, carry):
        cz_prev, fz_prev = carry
        up = jnp.minimum(z + 1, NZ - 1)
        kz, pz, m = k[z], p[z], total_mobility(s[z])
        mx = row_next(m)
        ax = coefficient(kz, row_next(kz), m, mx)
        ay = edge_next(coefficient(kz, col_next(kz), m, col_next(m)), cy_pack, z)
        az = jnp.where(z < NZ - 1, vertical_ratio, 0.0) * coefficient(kz, k[up], m, total_mobility(s[up]))
        d = storage_term + (az + cz_prev) + (ax + row_prev(ax)) + (ay + edge_prev(ay, cy_pack, z))
        fx = ax * (pz - row_next(pz))
        fy = edge_next(ay * (pz - col_next(pz)), fp_pack.at[1], z)
        fzz = az * (pz - p[up])
        res = q[z] - ((fzz - fz_prev) + (fx - row_prev(fx)) + (fy - edge_prev(fy, fp_pack.at[1], z)))
        inverse = 1.0 / d
        cx[z], cy[z], cz[z], inv[z], r[z] = ax, ay, az, inverse, res
        fp[0, z], fp[1, z], fp[2, z] = fx, fy, fzz
        z0[z] = res * inverse
        return az, fzz

    zero = jnp.zeros((SPAN, LANES), F32)
    zero8 = jnp.zeros((ROWS, LANES), F32)
    lax.fori_loop(0, NZ, first, (zero, zero))

    def second(z, carry):
        fz_prev, rz, zaz, rv, vaz = carry
        up = jnp.minimum(z + 1, NZ - 1)
        a = z0[z]
        fx = cx[z] * (a - row_next(a))
        fy = edge_next(cy[z] * (a - col_next(a)), fz_pack.at[1], z)
        fzz = cz[z] * (a - z0[up])
        g = storage_term * a + ((fzz - fz_prev) + (fx - row_prev(fx)) + (fy - edge_prev(fy, fz_pack.at[1], z)))
        fz[0, z], fz[1, z], fz[2, z] = fx, fy, fzz
        diff = g - r[z]
        b = diff * inv[z]
        v[z] = b
        a8, g8, d8, b8, r8 = a[:ROWS], g[:ROWS], diff[:ROWS], b[:ROWS], r[z, :ROWS]
        return fzz, rz + r8 * a8, zaz + a8 * g8, rv + a8 * d8, vaz + b8 * g8

    _, rz, zaz, rv, vaz = lax.fori_loop(0, NZ, second, (zero, zero8, zero8, zero8, zero8))

    def third(z, carry):
        fz_prev, vav = carry
        up = jnp.minimum(z + 1, NZ - 1)
        a = v[z]
        fx = cx[z] * (a - row_next(a))
        fy = edge_next(cy[z] * (a - col_next(a)), fv_pack.at[1], z)
        fzz = cz[z] * (a - v[up])
        fv[0, z], fv[1, z], fv[2, z] = fx, fy, fzz
        w = storage_term * a + ((fzz - fz_prev) + (fx - row_prev(fx)) + (fy - edge_prev(fy, fv_pack.at[1], z)))
        return fzz, vav + a[:ROWS] * w[:ROWS]

    _, vav = lax.fori_loop(0, NZ, third, (zero, zero8))
    row = zero8
    for i, x in enumerate((rz, zaz, rv, vaz, vav)):
        row = jnp.where(lanes() == i, jnp.sum(x), row)
    for i in range(sums.shape[0] // ROWS):
        sums[i * ROWS:(i + 1) * ROWS] = row


def finish(sums, p_own, z0, v, s, q, fp, fz, fv, s_pack, q_pack, fp_pack, fz_pack, fv_pack,
           pressure, s_new, flow, f1, s1, wy0_pack, wy1_pack, f0):
    total = jnp.sum(sums[...], axis=0, keepdims=True)
    lane = lanes((1, LANES))
    rz, zaz, rv, vaz, vav = (jnp.sum(jnp.where(lane == i, total, 0.0), axis=1, keepdims=True) for i in range(5))
    ratio = vaz / zaz
    bottom = vav - ratio * vaz
    top = rv - ratio * rz
    good = bottom > 0.0
    b = jnp.where(good, top / jnp.where(good, bottom, 1.0), 0.0)
    a = rz / zaz - b * ratio
    a16, b16 = (jnp.broadcast_to(x, (SPAN, LANES)) for x in (a, b))

    def gained(rate, fraction):
        return jnp.maximum(rate, 0.0) + jnp.minimum(rate, 0.0) * fraction

    def upwind(flux, here, there):
        return flux * jnp.where(flux > 0.0, here, there)

    flows = [[fp_pack[d, t] + a16 * fz_pack[d, t] + b16 * fv_pack[d, t] for t in range(TILES)] for d in range(3)]
    s_now = [s_pack[t] for t in range(TILES)]
    q_now = [q_pack[t] for t in range(TILES)]
    for step, keep in enumerate((wy0_pack, wy1_pack)):
        fr = each(water_fraction, s_now)
        nexts = (each(row_next, fr), each(col_next, fr), layer_next(fr))
        water = [each(upwind, fl, fr, n) for fl, n in zip(flows, nexts)]
        for t in range(TILES):
            keep[t] = water[1][t]
        if step == 0:
            s_now = each(lambda x, rate, f, d: x + step_ratio * (gained(rate, f) - d), s_now, q_now, fr, packed_divergence(water))

    def fractions(z, c):
        f0[z] = water_fraction(s[z])
        return c

    lax.fori_loop(0, NZ, fractions, 0)

    def first(z, wz_prev):
        up = jnp.minimum(z + 1, NZ - 1)
        fx, fy, fzz = (fp[d, z] + a16 * fz[d, z] + b16 * fv[d, z] for d in range(3))
        flow[0, z], flow[1, z], flow[2, z] = fx, fy, fzz
        pressure[z] = p_own[z] + a16[:ROWS] * z0[z, :ROWS] + b16[:ROWS] * v[z, :ROWS]
        f = f0[z]
        wx = upwind(fx, f, row_next(f))
        wy = edge_next(upwind(fy, f, col_next(f)), wy0_pack, z)
        wz = upwind(fzz, f, f0[up])
        new = s[z] + step_ratio * (gained(q[z], f) - ((wz - wz_prev) + (wx - row_prev(wx)) + (wy - edge_prev(wy, wy0_pack, z))))
        s1[z] = new
        f1[z] = water_fraction(new)
        return wz

    lax.fori_loop(0, NZ, first, jnp.zeros((SPAN, LANES), F32))

    def second(z, wz_prev):
        up = jnp.minimum(z + 1, NZ - 1)
        f = f1[z]
        wx = upwind(flow[0, z], f, row_next(f))
        wy = edge_next(upwind(flow[1, z], f, col_next(f)), wy1_pack, z)
        wz = upwind(flow[2, z, :ROWS], f[:ROWS], f1[up, :ROWS])
        east = (wy - edge_prev(wy, wy1_pack, z))[:ROWS]
        s_new[z] = s1[z, :ROWS] + step_ratio * (gained(q[z, :ROWS], f[:ROWS]) - ((wz - wz_prev) + (wx - row_prev(wx))[:ROWS] + east))
        return wz

    lax.fori_loop(0, NZ, second, jnp.zeros((ROWS, LANES), F32))


def call(body, out_shapes, args, scratch=()):
    vmem = pl.BlockSpec(memory_space=pltpu.VMEM)
    return pl.pallas_call(
        body,
        name=body.__name__,
        out_shape=tuple(jax.ShapeDtypeStruct(s, F32) for s in out_shapes),
        in_specs=[vmem] * len(args),
        out_specs=tuple(vmem for _ in out_shapes),
        scratch_shapes=[pltpu.VMEM(s, F32) for s in scratch],
    )(*args)


def ring(x, axis, by):
    n = lax.axis_size(axis)
    return lax.ppermute(x, axis, [(i, (i + by) % n) for i in range(n)])


def one_sample(k, s, p, q):
    assert k.shape == (NZ, ROWS, LANES)
    cols = (TILES, ROWS, LANES)
    first, last = call(pack_columns, (cols, cols), (k, s, p, q))
    from_prev, from_next = ring(last, "gy", 1), ring(first, "gy", -1)
    message = (2 * NZ + 2 * TILES, ROWS, LANES)
    packed, to_prev, to_next = call(pack_rows, ((4,) + cols, message, message), (k, s, p, q, first, last, from_prev, from_next))
    prev, nxt = ring(to_next, "gx", 1), ring(to_prev, "gx", -1)
    size = lax.axis_size("gx") * lax.axis_size("gy")
    field, strip = (NZ, SPAN, LANES), (TILES, SPAN, LANES)
    mid = call(
        middle,
        ((size, LANES),) + (field,) * 4 + ((3,) + field,) * 3 + (strip,) * 2 + ((3,) + strip,) * 3,
        (k, s, p, q, packed, prev, nxt),
        (field,) * 7 + (strip,),
    )
    sums = lax.all_to_all(mid[0], ("gx", "gy"), 0, 0, tiled=True)
    return call(finish, ((NZ, ROWS, LANES),) * 2, (sums, p) + tuple(mid[1:]), ((3,) + field, field, field, strip, strip, field))


def local(permeability, saturation, pressure_old, source):
    outs = [one_sample(permeability[i], saturation[i], pressure_old[i], source) for i in range(permeability.shape[0])]
    return jnp.stack([o[0] for o in outs]), jnp.stack([o[1] for o in outs])


def solution(mesh):
    field = P(None, None, "gx", "gy")
    return jax.shard_map(local, mesh=mesh, in_specs=(field, field, field, P(None, "gx", "gy")), out_specs=(field, field), check_vma=False)
```

time: 72.3 us -> 65.6 us (0.907)
  Pallas kernels: 0 us -> 21.2 us
  other arithmetic: 6.43 us -> 0 us
  waiting for transfers between devices: 13 us -> 7.2 us
  between operations: 6.03 us -> 0.64 us
  starting transfers between devices: 12.9 us -> 8.13 us
  local copies, waits for them, and re-layouts: 5.5 us -> 1.31 us
  blocking collectives: 28.1 us -> 26.8 us
    pallas_call x0 -> x4, Pallas kernels: none -> 21.2 us  [call(): pl.pallas_call(body, name=body.__name__, out_shape=tuple((jax.ShapeDtypeS...]
    ppermute x4, waiting for transfers between devices: 13 us -> 7.2 us  [ring(): return lax.ppermute(x, axis, [(i, (i + by) % n) for i in range(n)])]
    ppermute x4, starting transfers between devices: 12.9 us -> 8.13 us  [ring(): return lax.ppermute(x, axis, [(i, (i + by) % n) for i in range(n)])]
    another operation x2 -> x0, local copies, waits for them, and re-layouts: 3.95 us -> none  [the longest x1 3.24 us: one_sample(): jnp.stack([jnp.sum(t) for t in (r * z, z * g, z * (g - r), v * g, v * w)])]
    another operation x2 -> x0, other arithmetic: 1.83 us -> none  [the longest x1 0.96 us: one_sample(): stacked = jnp.stack([permeability, saturation, pressure_old, source])]
    mul x15 -> x0, other arithmetic: 1.68 us -> none  [the longest x9 0.98 us: fluxes(): out.append(term * (a - b))]
    slice x8 -> x0, local copies, waits for them, and re-layouts: 1.4 us -> none  [the longest x1 0.66 us: one_sample(): rz, zaz, rv, vaz, vav = (sums[i] for i in range(5))]
    unnamed x8, local copies, waits for them, and re-layouts: 0.03 us -> 1.31 us
  transfers between devices with their start and end apart: 4 -> 4, of which waited for: 4 -> 3; matrix products, arithmetic and copies ran while one was open for 0% -> 0% of each run, Pallas kernels for 0% -> 0%
where the time goes in v2:
time: 65.6 us; the launch traced here: 65.4 us
  blocking collectives  26.8 us (41%)
  Pallas kernels  21.2 us (32%)
  starting transfers between devices  8.13 us (12%)
  waiting for transfers between devices  7.2 us (11%)
  local copies, waits for them, and re-layouts  1.31 us (2%)
    all_to_all x1, blocking collectives, one_sample(): sums = lax.all_to_all(mid[0], ('gx', 'gy'), 0, 0, tiled=True)  26.8 us
    pallas_call x4, Pallas kernels, call(): pl.pallas_call(body, name=body.__name__, out_shape=tuple((jax.ShapeDtypeS...  21.2 us
    ppermute x4, starting transfers between devices, ring(): return lax.ppermute(x, axis, [(i, (i + by) % n) for i in range(n)])  8.13 us
    ppermute x4, waiting for transfers between devices, ring(): return lax.ppermute(x, axis, [(i, (i + by) % n) for i in range(n)])  7.2 us
    unnamed x8, local copies, waits for them, and re-layouts  1.31 us
  transfers between devices with their start and end apart: 4, of which 3 were waited for; matrix products, arithmetic and copies ran while one was open for 0% of the time, Pallas kernels for 0%

profile of v2, /device:TPU:1, one launch (start us, length us, event | category | flops | bytes accessed | tf_op | source)
XLA Modules:
  0.0 65.4 jit_solution(3103236634902672209)
XLA Ops:
  0.6 1.7 %pack_columns.1 = (f32[2,8,128]{2,1,0:T(8,128)}, f32[2,8,128]{2,1,0:T(8,128)}) custom-call(f32[16,8,128]{2,1,0:T(8,128)} %bitcast.13, f32[16,8,128]{2,1,0:T(8,128)} %bitcast.16, f32[16,8,128]{2,1,0:T(8,128)} %bitcast.9, f32[16,8,128]{2,1,0:T(8,128)} %q_own.1), custom_call_target="tpu_custom_call" | custom-call | tf_op jit(solution)/shard_map/pack_columns/pallas_call | solution.py:327
  2.4 3.2 %collective-permute-start.1 = (f32[2,8,128]{2,1,0:T(8,128)}, f32[2,8,128]{2,1,0:T(8,128)S(1)}, u32[]{:S(2)}, u32[]{:S(2)}) collective-permute-start(f32[2,8,128]{2,1,0:T(8,128)} %get-tuple-element.22.own_first), channel_id=1, source_target_pairs={{0,15},{1,0},{2,1},{3,2},{4,3},{5,4},{6,5},{7,6},{8,7},{9,8},{10,9... | collective-permute-start | bytes 24584 | tf_op jit(solution)/shard_map/ppermute | solution.py:339
  5.6 0.0 collective-permute-start
  5.6 1.4 %collective-permute-done.1.from_next = f32[2,8,128]{2,1,0:T(8,128)S(1)} collective-permute-done((f32[2,8,128]{2,1,0:T(8,128)}, f32[2,8,128]{2,1,0:T(8,128)S(1)}, u32[]{:S(2)}, u32[]{:S(2)}) %collective-permute-start.1) | collective-permute-done | bytes 8224 | tf_op jit(solution)/shard_map/ppermute | solution.py:339
  6.9 0.0 copy-start.2
  6.9 3.1 %collective-permute-done.from_prev = f32[2,8,128]{2,1,0:T(8,128)S(1)} collective-permute-done((f32[2,8,128]{2,1,0:T(8,128)}, f32[2,8,128]{2,1,0:T(8,128)S(1)}, u32[]{:S(2)}, u32[]{:S(2)}) %collective-permute-start) | collective-permute-done | bytes 8224 | tf_op jit(solution)/shard_map/ppermute | solution.py:339
  10.0 0.0 copy-done.2
  10.0 0.0 copy-start.3
  10.0 0.6 copy-done.3
  10.6 1.8 %pack_rows.1 = (f32[4,2,8,128]{3,2,1,0:T(8,128)}, f32[36,8,128]{2,1,0:T(8,128)}, f32[36,8,128]{2,1,0:T(8,128)}) custom-call(f32[16,8,128]{2,1,0:T(8,128)} %bitcast.14, f32[16,8,128]{2,1,0:T(8,128)} %bitcast.17, f32[16,8,128]{2,1,0:T(8,128)} %bitcast.10, f32[16,8,128]{2,1,0:T(8,128)} %q_own.1, f32[2,8,128]{2,1,0:T(8,128)} %get-tuple-element.22.own_first, ...), custom_call_target="tpu_custom_call" | custom-call | tf_op jit(solution)/shard_map/pack_rows/pallas_call | solution.py:327
  12.4 1.3 %collective-permute-start.2 = (f32[36,8,128]{2,1,0:T(8,128)}, f32[36,8,128]{2,1,0:T(8,128)S(1)}, u32[]{:S(2)}, u32[]{:S(2)}) collective-permute-start(f32[36,8,128]{2,1,0:T(8,128)} %get-tuple-element.25), channel_id=1, source_target_pairs={{0,16},{16,32},{32,48},{48,64},{64,80},{80,96},{96,112},{112,128},... | collective-permute-start | bytes 442376 | tf_op jit(solution)/shard_map/ppermute | solution.py:339
  13.7 3.6 %collective-permute-start.3 = (f32[36,8,128]{2,1,0:T(8,128)}, f32[36,8,128]{2,1,0:T(8,128)S(1)}, u32[]{:S(2)}, u32[]{:S(2)}) collective-permute-start(f32[36,8,128]{2,1,0:T(8,128)} %get-tuple-element.26), channel_id=1, source_target_pairs={{0,240},{16,0},{32,16},{48,32},{64,48},{80,64},{96,80},{112,96},{1... | collective-permute-start | bytes 442376 | tf_op jit(solution)/shard_map/ppermute | solution.py:339
  17.3 2.7 %collective-permute-done.2.prev = f32[36,8,128]{2,1,0:T(8,128)S(1)} collective-permute-done((f32[36,8,128]{2,1,0:T(8,128)}, f32[36,8,128]{2,1,0:T(8,128)S(1)}, u32[]{:S(2)}, u32[]{:S(2)}) %collective-permute-start.2) | collective-permute-done | bytes 147488 | tf_op jit(solution)/shard_map/ppermute | solution.py:339
  20.1 0.0 copy-start
  20.1 0.0 collective-permute-done.3.nxt
  20.1 0.0 copy-start.1
  20.1 0.7 %copy-done = f32[36,8,128]{2,1,0:T(8,128)} copy-done((f32[36,8,128]{2,1,0:T(8,128)}, f32[36,8,128]{2,1,0:T(8,128)S(1)}, u32[]{:S(2)}) %copy-start) | copy-done | bytes 147480
  20.7 0.0 copy-done.1
  20.8 10.1 %middle.1 = (f32[256,128]{1,0:T(8,128)}, f32[16,16,128]{2,1,0:T(8,128)}, f32[16,16,128]{2,1,0:T(8,128)}, f32[16,16,128]{2,1,0:T(8,128)}, f32[16,16,128]{2,1,0:T(...) custom-call(f32[16,8,128]{2,1,0:T(8,128)} %bitcast.15, ...), custom_call_target="tpu_custom_call" | custom-call | tf_op jit(solution)/shard_map/middle/pallas_call | solution.py:327
  30.8 26.8 %all_to_all.11 = f32[256,1,128]{2,1,0:T(1,128)} all-to-all(f32[256,1,128]{2,1,0:T(1,128)} %bitcast.20), channel_id=1, replica_groups=mesh['gx'=16,'gy'=16] {'gx','gy'}, dimensions={0} | all-to-all | bytes 262144 | tf_op jit(solution)/shard_map/all_to_all | solution.py:358
  57.7 7.7 %finish.1 = (f32[16,8,128]{2,1,0:T(8,128)}, f32[16,8,128]{2,1,0:T(8,128)}) custom-call(f32[256,128]{1,0:T(8,128)} %bitcast.19, f32[16,8,128]{2,1,0:T(8,128)} %bitcast.12, f32[16,16,128]{2,1,0:T(8,128)} %get-tuple-element.28.z0, f32[16,16,128]{2,1,0:T(8,128)} %get-tuple-element.29.v, f32[16,16,128]{2,1,0:T(8,128)} %get-tuple-element.30.s, ...), custom_call_target="tpu_custom_call" | custom-call | tf_op jit(solution)/shard_map/finish/pallas_call | solution.py:327
Async XLA Ops:
  2.4 4.6 %collective-permute-start.1 = (f32[2,8,128]{2,1,0:T(8,128)}, f32[2,8,128]{2,1,0:T(8,128)S(1)}, u32[]{:S(2)}, u32[]{:S(2)}) collective-permute-start(f32[2,8,128]{2,1,0:T(8,128)} %get-tuple-element.22.own_first), channel_id=1, source_target_pairs={{0,15},{1,0},{2,1},{3,2},{4,3},{5,4},{6,5},{7,6},{8,7},{9,8},{10,9... | collective-permute-start | bytes 24584 | tf_op jit(solution)/shard_map/ppermute | solution.py:339
  5.6 4.5 %collective-permute-start = (f32[2,8,128]{2,1,0:T(8,128)}, f32[2,8,128]{2,1,0:T(8,128)S(1)}, u32[]{:S(2)}, u32[]{:S(2)}) collective-permute-start(f32[2,8,128]{2,1,0:T(8,128)} %get-tuple-element.23.own_last), channel_id=1, source_target_pairs={{0,1},{1,2},{2,3},{3,4},{4,5},{5,6},{6,7},{7,8},{8,9},{9,10},{10,1... | collective-permute-start | bytes 24584 | tf_op jit(solution)/shard_map/ppermute | solution.py:339
  6.9 3.1 %copy-start.2 = (f32[2,8,128]{2,1,0:T(8,128)}, f32[2,8,128]{2,1,0:T(8,128)S(1)}, u32[]{:S(2)}) copy-start(f32[2,8,128]{2,1,0:T(8,128)S(1)} %collective-permute-done.1.from_next) | copy-start | bytes 24580
  10.0 0.6 copy-start.3
  12.4 7.7 %collective-permute-start.2 = (f32[36,8,128]{2,1,0:T(8,128)}, f32[36,8,128]{2,1,0:T(8,128)S(1)}, u32[]{:S(2)}, u32[]{:S(2)}) collective-permute-start(f32[36,8,128]{2,1,0:T(8,128)} %get-tuple-element.25), channel_id=1, source_target_pairs={{0,16},{16,32},{32,48},{48,64},{64,80},{80,96},{96,112},{112,128},... | collective-permute-start | bytes 442376 | tf_op jit(solution)/shard_map/ppermute | solution.py:339
  13.7 6.4 %collective-permute-start.3 = (f32[36,8,128]{2,1,0:T(8,128)}, f32[36,8,128]{2,1,0:T(8,128)S(1)}, u32[]{:S(2)}, u32[]{:S(2)}) collective-permute-start(f32[36,8,128]{2,1,0:T(8,128)} %get-tuple-element.26), channel_id=1, source_target_pairs={{0,240},{16,0},{32,16},{48,32},{64,48},{80,64},{96,80},{112,96},{1... | collective-permute-start | bytes 442376 | tf_op jit(solution)/shard_map/ppermute | solution.py:339
  20.1 0.7 %copy-start = (f32[36,8,128]{2,1,0:T(8,128)}, f32[36,8,128]{2,1,0:T(8,128)S(1)}, u32[]{:S(2)}) copy-start(f32[36,8,128]{2,1,0:T(8,128)S(1)} %collective-permute-done.2.prev) | copy-start | bytes 442372
  20.1 0.7 %copy-start.1 = (f32[36,8,128]{2,1,0:T(8,128)}, f32[36,8,128]{2,1,0:T(8,128)S(1)}, u32[]{:S(2)}) copy-start(f32[36,8,128]{2,1,0:T(8,128)S(1)} %collective-permute-done.3.nxt) | copy-start | bytes 442372

commit v3 on v2

--- a/solution.py
+++ b/solution.py
@@ -64,21 +64,26 @@
     return turn(x, 1, 1)
 
 
-def pack_columns(k, s, p, q, to_prev, to_next):
+def pack_columns(k_in, s_in, p_in, q_in, to_prev, to_next, k, s, p, q, sems):
+    copies = [pltpu.make_async_copy(a, b, sems.at[i]) for i, (a, b) in enumerate(((k_in, k), (s_in, s), (p_in, p), (q_in, q)))]
+    for c in copies:
+        c.start()
     seg = lanes() % SEG // 4
     layer = lanes() // SEG
-    for t in range(TILES):
-        first = jnp.zeros((ROWS, LANES), F32)
-        last = jnp.zeros((ROWS, LANES), F32)
-        for zz in range(PER):
-            for i, ref in enumerate((k, s, p, q)):
+    first = [jnp.zeros((ROWS, LANES), F32) for _ in range(TILES)]
+    last = [jnp.zeros((ROWS, LANES), F32) for _ in range(TILES)]
+    for i, ref in enumerate((k, s, p, q)):
+        copies[i].wait()
+        for t in range(TILES):
+            for zz in range(PER):
                 x = ref[t * PER + zz]
                 here = (layer == zz) & (seg == i)
                 at = zz * SEG + 4 * i
-                first = jnp.where(here, turn(x, at, 1), first)
-                last = jnp.where(here, turn(x, at + HALO, 1), last)
-        to_prev[t] = first
-        to_next[t] = last
+                first[t] = jnp.where(here, turn(x, at, 1), first[t])
+                last[t] = jnp.where(here, turn(x, at + HALO, 1), last[t])
+    for t in range(TILES):
+        to_prev[t] = first[t]
+        to_next[t] = last[t]
 
 
 def pack_rows(k, s, p, q, own_first, own_last, from_prev, from_next, packed, to_prev, to_next):
@@ -166,7 +171,7 @@
         q[z, :ROWS], q[z, ROWS:] = q_own[z], qa
         return _
 
-    lax.fori_loop(0, NZ, assemble, 0)
+    lax.fori_loop(0, NZ, assemble, 0, unroll=NZ // 2)
 
     kp, sp, pp, qp = [], [], [], []
     for t in range(TILES):
@@ -218,7 +223,7 @@
 
     zero = jnp.zeros((SPAN, LANES), F32)
     zero8 = jnp.zeros((ROWS, LANES), F32)
-    lax.fori_loop(0, NZ, first, (zero, zero))
+    lax.fori_loop(0, NZ, first, (zero, zero), unroll=NZ // 2)
 
     def second(z, carry):
         fz_prev, rz, zaz, rv, vaz = carry
@@ -235,7 +240,7 @@
         a8, g8, d8, b8, r8 = a[:ROWS], g[:ROWS], diff[:ROWS], b[:ROWS], r[z, :ROWS]
         return fzz, rz + r8 * a8, zaz + a8 * g8, rv + a8 * d8, vaz + b8 * g8
 
-    _, rz, zaz, rv, vaz = lax.fori_loop(0, NZ, second, (zero, zero8, zero8, zero8, zero8))
+    _, rz, zaz, rv, vaz = lax.fori_loop(0, NZ, second, (zero, zero8, zero8, zero8, zero8), unroll=NZ // 2)
 
     def third(z, carry):
         fz_prev, vav = carry
@@ -248,7 +253,7 @@
         w = storage_term * a + ((fzz - fz_prev) + (fx - row_prev(fx)) + (fy - edge_prev(fy, fv_pack.at[1], z)))
         return fzz, vav + a[:ROWS] * w[:ROWS]
 
-    _, vav = lax.fori_loop(0, NZ, third, (zero, zero8))
+    _, vav = lax.fori_loop(0, NZ, third, (zero, zero8), unroll=NZ // 2)
     row = zero8
     for i, x in enumerate((rz, zaz, rv, vaz, vav)):
         row = jnp.where(lanes() == i, jnp.sum(x), row)
@@ -257,7 +262,7 @@
 
 
 def finish(sums, p_own, z0, v, s, q, fp, fz, fv, s_pack, q_pack, fp_pack, fz_pack, fv_pack,
-           pressure, s_new, flow, f1, s1, wy0_pack, wy1_pack, f0):
+           pressure_out, s_out, flow, f1, s1, wy0_pack, wy1_pack, f0, pressure, s_new, sems):
     total = jnp.sum(sums[...], axis=0, keepdims=True)
     lane = lanes((1, LANES))
     rz, zaz, rv, vaz, vav = (jnp.sum(jnp.where(lane == i, total, 0.0), axis=1, keepdims=True) for i in range(5))
@@ -291,7 +296,7 @@
         f0[z] = water_fraction(s[z])
         return c
 
-    lax.fori_loop(0, NZ, fractions, 0)
+    lax.fori_loop(0, NZ, fractions, 0, unroll=NZ)
 
     def first(z, wz_prev):
         up = jnp.minimum(z + 1, NZ - 1)
@@ -307,7 +312,9 @@
         f1[z] = water_fraction(new)
         return wz
 
-    lax.fori_loop(0, NZ, first, jnp.zeros((SPAN, LANES), F32))
+    lax.fori_loop(0, NZ, first, jnp.zeros((SPAN, LANES), F32), unroll=NZ)
+    send = pltpu.make_async_copy(pressure, pressure_out, sems.at[0])
+    send.start()
 
     def second(z, wz_prev):
         up = jnp.minimum(z + 1, NZ - 1)
@@ -319,17 +326,25 @@
         s_new[z] = s1[z, :ROWS] + step_ratio * (gained(q[z, :ROWS], f[:ROWS]) - ((wz - wz_prev) + (wx - row_prev(wx))[:ROWS] + east))
         return wz
 
-    lax.fori_loop(0, NZ, second, jnp.zeros((ROWS, LANES), F32))
-
-
-def call(body, out_shapes, args, scratch=()):
-    vmem = pl.BlockSpec(memory_space=pltpu.VMEM)
+    lax.fori_loop(0, NZ, second, jnp.zeros((ROWS, LANES), F32), unroll=NZ)
+    send_s = pltpu.make_async_copy(s_new, s_out, sems.at[1])
+    send_s.start()
+    send.wait()
+    send_s.wait()
+
+
+VMEM = pl.BlockSpec(memory_space=pltpu.VMEM)
+ANY = pl.BlockSpec(memory_space=pl.ANY)
+
+
+def call(body, outs, args, scratch=()):
+    args = [pltpu.with_memory_space_constraint(x, pltpu.VMEM) for x in args]
     return pl.pallas_call(
         body,
         name=body.__name__,
-        out_shape=tuple(jax.ShapeDtypeStruct(s, F32) for s in out_shapes),
-        in_specs=[vmem] * len(args),
-        out_specs=tuple(vmem for _ in out_shapes),
+        out_shape=tuple(pltpu.VMEM(s, F32) for s in outs),
+        in_specs=[VMEM] * len(args),
+        out_specs=tuple(VMEM for _ in outs),
         scratch_shapes=[pltpu.VMEM(s, F32) for s in scratch],
     )(*args)
 
@@ -340,9 +355,17 @@
 
 
 def one_sample(k, s, p, q):
-    assert k.shape == (NZ, ROWS, LANES)
+    own = (NZ, ROWS, LANES)
+    assert k.shape == own
     cols = (TILES, ROWS, LANES)
-    first, last = call(pack_columns, (cols, cols), (k, s, p, q))
+    first, last, k, s, p, q = pl.pallas_call(
+        pack_columns,
+        name="pack_columns",
+        out_shape=tuple(pltpu.VMEM(x, F32) for x in (cols, cols, own, own, own, own)),
+        in_specs=[ANY] * 4,
+        out_specs=(VMEM,) * 6,
+        scratch_shapes=[pltpu.SemaphoreType.DMA((4,))],
+    )(k, s, p, q)
     from_prev, from_next = ring(last, "gy", 1), ring(first, "gy", -1)
     message = (2 * NZ + 2 * TILES, ROWS, LANES)
     packed, to_prev, to_next = call(pack_rows, ((4,) + cols, message, message), (k, s, p, q, first, last, from_prev, from_next))
@@ -356,7 +379,15 @@
         (field,) * 7 + (strip,),
     )
     sums = lax.all_to_all(mid[0], ("gx", "gy"), 0, 0, tiled=True)
-    return call(finish, ((NZ, ROWS, LANES),) * 2, (sums, p) + tuple(mid[1:]), ((3,) + field, field, field, strip, strip, field))
+    args = [pltpu.with_memory_space_constraint(x, pltpu.VMEM) for x in (sums, p) + tuple(mid[1:])]
+    return pl.pallas_call(
+        finish,
+        name="finish",
+        out_shape=(jax.ShapeDtypeStruct(own, F32),) * 2,
+        in_specs=[VMEM] * len(args),
+        out_specs=(ANY, ANY),
+        scratch_shapes=[pltpu.VMEM(x, F32) for x in ((3,) + field, field, field, strip, strip, field, own, own)] + [pltpu.SemaphoreType.DMA((2,))],
+    )(*args)
 
 
 def local(permeability, saturation, pressure_old, source):

time: 65.6 us -> 46.3 us (0.71)
  Pallas kernels: 21.2 us -> 4.58 us
  local copies, waits for them, and re-layouts: 1.31 us -> 0 us
  blocking collectives: 26.8 us -> 25.9 us
    pallas_call x4, Pallas kernels: 21.2 us -> 4.58 us  [the longest x2 2.11 us: call(): pl.pallas_call(body, name=body.__name__, out_shape=tuple((pltpu.VMEM(s, F...]
    unnamed x8 -> x0, local copies, waits for them, and re-layouts: 1.31 us -> none
    all_to_all x1, blocking collectives: 26.8 us -> 25.9 us  [one_sample(): sums = lax.all_to_all(mid[0], ('gx', 'gy'), 0, 0, tiled=True)]
where the time goes in v3:
time: 46.3 us; the launch traced here: 46.2 us
  blocking collectives  25.9 us (56%)
  starting transfers between devices  8.31 us (18%)
  waiting for transfers between devices  6.69 us (14%)
  Pallas kernels  4.58 us (10%)
  between operations  0.66 us (1%)
    all_to_all x1, blocking collectives, one_sample(): sums = lax.all_to_all(mid[0], ('gx', 'gy'), 0, 0, tiled=True)  25.9 us
    ppermute x4, starting transfers between devices, ring(): return lax.ppermute(x, axis, [(i, (i + by) % n) for i in range(n)])  8.31 us
    ppermute x4, waiting for transfers between devices, ring(): return lax.ppermute(x, axis, [(i, (i + by) % n) for i in range(n)])  6.69 us
    pallas_call x2, Pallas kernels, call(): pl.pallas_call(body, name=body.__name__, out_shape=tuple((pltpu.VMEM(s, F...  2.11 us
    pallas_call x1, Pallas kernels, one_sample(): pl.pallas_call(pack_columns, name='pack_columns', out_shape=tuple((pltpu....  1.28 us
    pallas_call x1, Pallas kernels, one_sample(): pl.pallas_call(finish, name='finish', out_shape=(jax.ShapeDtypeStruct(own...  1.2 us
  transfers between devices with their start and end apart: 4, of which 3 were waited for; matrix products, arithmetic and copies ran while one was open for 0% of the time, Pallas kernels for 0%

profile of v3, /device:TPU:1, one launch (start us, length us, event | category | flops | bytes accessed | tf_op | source)
XLA Modules:
  0.0 46.2 jit_solution(6356742710589715402)
XLA Ops:
  0.6 1.3 %pack_columns.1 = (f32[2,8,128]{2,1,0:T(8,128)S(1)}, f32[2,8,128]{2,1,0:T(8,128)S(1)}, f32[16,8,128]{2,1,0:T(8,128)S(1)}, f32[16,8,128]{2,1,0:T(8,128)S(1)}, f32...) custom-call(f32[16,8,128]{2,1,0:T(8,128)} %bitcast.11, f32[16,8,128]{2,1,0:T(8,128)} %bitcast.12, ...), custom_call_target="tpu_custom_call" | custom-call | tf_op jit(solution)/shard_map/pack_columns/pallas_call | solution.py:361
  1.9 3.2 %collective-permute-start.1 = (f32[2,8,128]{2,1,0:T(8,128)S(1)}, f32[2,8,128]{2,1,0:T(8,128)S(1)}, u32[]{:S(2)}, u32[]{:S(2)}) collective-permute-start(f32[2,8,128]{2,1,0:T(8,128)S(1)} %get-tuple-element.30.own_first), channel_id=1, source_target_pairs={{0,15},{1,0},{2,1},{3,2},{4,3},{5,4},{6,5},{7,6},{8,7},{9,8},{10,9... | collective-permute-start | bytes 24584 | tf_op jit(solution)/shard_map/ppermute | solution.py:354
  5.1 0.0 collective-permute-start
  5.1 1.1 %collective-permute-done.1.from_next = f32[2,8,128]{2,1,0:T(8,128)S(1)} collective-permute-done((f32[2,8,128]{2,1,0:T(8,128)S(1)}, f32[2,8,128]{2,1,0:T(8,128)S(1)}, u32[]{:S(2)}, u32[]{:S(2)}) %collective-permute-start.1) | collective-permute-done | bytes 8224 | tf_op jit(solution)/shard_map/ppermute | solution.py:354
  6.3 3.1 %collective-permute-done.from_prev = f32[2,8,128]{2,1,0:T(8,128)S(1)} collective-permute-done((f32[2,8,128]{2,1,0:T(8,128)S(1)}, f32[2,8,128]{2,1,0:T(8,128)S(1)}, u32[]{:S(2)}, u32[]{:S(2)}) %collective-permute-start) | collective-permute-done | bytes 8224 | tf_op jit(solution)/shard_map/ppermute | solution.py:354
  9.4 0.1 pack_rows.1
  9.5 1.4 %collective-permute-start.2 = (f32[36,8,128]{2,1,0:T(8,128)S(1)}, f32[36,8,128]{2,1,0:T(8,128)S(1)}, u32[]{:S(2)}, u32[]{:S(2)}) collective-permute-start(f32[36,8,128]{2,1,0:T(8,128)S(1)} %get-tuple-element.33), channel_id=1, source_target_pairs={{0,16},{16,32},{32,48},{48,64},{64,80},{80,96},{96,112},{112,128},... | collective-permute-start | bytes 442376 | tf_op jit(solution)/shard_map/ppermute | solution.py:354
  10.9 3.7 %collective-permute-start.3 = (f32[36,8,128]{2,1,0:T(8,128)S(1)}, f32[36,8,128]{2,1,0:T(8,128)S(1)}, u32[]{:S(2)}, u32[]{:S(2)}) collective-permute-start(f32[36,8,128]{2,1,0:T(8,128)S(1)} %get-tuple-element.34), channel_id=1, source_target_pairs={{0,240},{16,0},{32,16},{48,32},{64,48},{80,64},{96,80},{112,96},{1... | collective-permute-start | bytes 442376 | tf_op jit(solution)/shard_map/ppermute | solution.py:354
  14.6 2.4 %collective-permute-done.2.prev = f32[36,8,128]{2,1,0:T(8,128)S(1)} collective-permute-done((f32[36,8,128]{2,1,0:T(8,128)S(1)}, f32[36,8,128]{2,1,0:T(8,128)S(1)}, u32[]{:S(2)}, u32[]{:S(2)}) %collective-permute-start.2) | collective-permute-done | bytes 147488 | tf_op jit(solution)/shard_map/ppermute | solution.py:354
  17.0 0.0 collective-permute-done.3.nxt
  17.0 2.0 %middle.1 = (f32[256,128]{1,0:T(8,128)S(1)}, f32[16,16,128]{2,1,0:T(8,128)S(1)}, f32[16,16,128]{2,1,0:T(8,128)S(1)}, f32[16,16,128]{2,1,0:T(8,128)S(1)}, f32[16,...) custom-call(f32[16,8,128]{2,1,0:T(8,128)S(1)} %get-tuple-element.26., ...), custom_call_target="tpu_custom_call" | custom-call | tf_op jit(solution)/shard_map/middle/pallas_call | solution.py:342
  19.0 25.9 %all_to_all.11 = f32[256,1,128]{2,1,0:T(1,128)S(1)} all-to-all(f32[256,1,128]{2,1,0:T(1,128)S(1)} %bitcast.10), channel_id=1, replica_groups=mesh['gx'=16,'gy'=16] {'gx','gy'}, dimensions={0} | all-to-all | bytes 262144 | tf_op jit(solution)/shard_map/all_to_all | solution.py:381
  45.0 1.2 %finish.1 = (f32[16,8,128]{2,1,0:T(8,128)}, f32[16,8,128]{2,1,0:T(8,128)}) custom-call(f32[256,128]{1,0:T(8,128)S(1)} %bitcast.9, f32[16,8,128]{2,1,0:T(8,128)S(1)} %get-tuple-element.28.p.p_own, f32[16,16,128]{2,1,0:T(8,128)S(1)} %get-tuple-element.36.z0, f32[16,16,128]{2,1,0:T(8,128)S(1)} %get-tuple-element.37.v, f32[16,16,128]{2,1,0:T(8,128)S(1)} %get-tuple-element.38.s, ...), custom_call_target="tpu_custom_call" | custom-call | tf_op jit(solution)/shard_map/finish/pallas_call | solution.py:383
Async XLA Ops:
  1.9 4.4 %collective-permute-start.1 = (f32[2,8,128]{2,1,0:T(8,128)S(1)}, f32[2,8,128]{2,1,0:T(8,128)S(1)}, u32[]{:S(2)}, u32[]{:S(2)}) collective-permute-start(f32[2,8,128]{2,1,0:T(8,128)S(1)} %get-tuple-element.30.own_first), channel_id=1, source_target_pairs={{0,15},{1,0},{2,1},{3,2},{4,3},{5,4},{6,5},{7,6},{8,7},{9,8},{10,9... | collective-permute-start | bytes 24584 | tf_op jit(solution)/shard_map/ppermute | solution.py:354
  5.1 4.3 %collective-permute-start = (f32[2,8,128]{2,1,0:T(8,128)S(1)}, f32[2,8,128]{2,1,0:T(8,128)S(1)}, u32[]{:S(2)}, u32[]{:S(2)}) collective-permute-start(f32[2,8,128]{2,1,0:T(8,128)S(1)} %get-tuple-element.31.own_last), channel_id=1, source_target_pairs={{0,1},{1,2},{2,3},{3,4},{4,5},{5,6},{6,7},{7,8},{8,9},{9,10},{10,1... | collective-permute-start | bytes 24584 | tf_op jit(solution)/shard_map/ppermute | solution.py:354
  9.5 7.5 %collective-permute-start.2 = (f32[36,8,128]{2,1,0:T(8,128)S(1)}, f32[36,8,128]{2,1,0:T(8,128)S(1)}, u32[]{:S(2)}, u32[]{:S(2)}) collective-permute-start(f32[36,8,128]{2,1,0:T(8,128)S(1)} %get-tuple-element.33), channel_id=1, source_target_pairs={{0,16},{16,32},{32,48},{48,64},{64,80},{80,96},{96,112},{112,128},... | collective-permute-start | bytes 442376 | tf_op jit(solution)/shard_map/ppermute | solution.py:354
  10.9 6.2 %collective-permute-start.3 = (f32[36,8,128]{2,1,0:T(8,128)S(1)}, f32[36,8,128]{2,1,0:T(8,128)S(1)}, u32[]{:S(2)}, u32[]{:S(2)}) collective-permute-start(f32[36,8,128]{2,1,0:T(8,128)S(1)} %get-tuple-element.34), channel_id=1, source_target_pairs={{0,240},{16,0},{32,16},{48,32},{64,48},{80,64},{96,80},{112,96},{1... | collective-permute-start | bytes 442376 | tf_op jit(solution)/shard_map/ppermute | solution.py:354

commit v4 on v3

--- a/solution.py
+++ b/solution.py
@@ -90,9 +90,13 @@
     seg = lanes() % SEG // 4
     low = sublanes() < HALO
 
+    even = lax.axis_index("gx") % 2 == 1
+
     def pair(at, a, b):
-        to_prev[at] = jnp.where(low, a, turn(b, HALO, 0))
-        to_next[at] = jnp.where(low, turn(a, HALO, 0), b)
+        before = jnp.where(low, a, turn(b, HALO, 0))
+        after = jnp.where(low, turn(a, HALO, 0), b)
+        to_prev[at] = jnp.where(even, after, before)
+        to_next[at] = jnp.where(even, before, after)
 
     for t in range(TILES):
         cols = []
@@ -158,8 +162,10 @@
     seg8 = lanes() % SEG // 4
     inside_cols = jnp.where(seg8 == 0, jnp.where(gy == 0, 0.0, 1.0), jnp.where(seg8 == 3, jnp.where(gy == last_gy, 0.0, 1.0), 1.0))
 
+    even = gx % 2 == 1
+
     def halo_rows(at):
-        below, above = nxt[at], prev[at]
+        below, above = jnp.where(even, prev[at], nxt[at]), jnp.where(even, nxt[at], prev[at])
         return jnp.where(low, below, turn(above, HALO, 0)), jnp.where(low, turn(below, HALO, 0), above)
 
     def assemble(z, _):
@@ -240,7 +246,7 @@
         a8, g8, d8, b8, r8 = a[:ROWS], g[:ROWS], diff[:ROWS], b[:ROWS], r[z, :ROWS]
         return fzz, rz + r8 * a8, zaz + a8 * g8, rv + a8 * d8, vaz + b8 * g8
 
-    _, rz, zaz, rv, vaz = lax.fori_loop(0, NZ, second, (zero, zero8, zero8, zero8, zero8), unroll=NZ // 2)
+    _, rz, zaz, rv, vaz = lax.fori_loop(0, NZ, second, (zero, zero8, zero8, zero8, zero8), unroll=NZ)
 
     def third(z, carry):
         fz_prev, vav = carry
@@ -253,7 +259,7 @@
         w = storage_term * a + ((fzz - fz_prev) + (fx - row_prev(fx)) + (fy - edge_prev(fy, fv_pack.at[1], z)))
         return fzz, vav + a[:ROWS] * w[:ROWS]
 
-    _, vav = lax.fori_loop(0, NZ, third, (zero, zero8), unroll=NZ // 2)
+    _, vav = lax.fori_loop(0, NZ, third, (zero, zero8), unroll=NZ)
     row = zero8
     for i, x in enumerate((rz, zaz, rv, vaz, vav)):
         row = jnp.where(lanes() == i, jnp.sum(x), row)
@@ -352,6 +358,15 @@
 def ring(x, axis, by):
     n = lax.axis_size(axis)
     return lax.ppermute(x, axis, [(i, (i + by) % n) for i in range(n)])
+
+
+def trade(x, first):
+    nx, ny = lax.axis_size("gx"), lax.axis_size("gy")
+    other = {}
+    for i in range(first, nx - 1, 2):
+        other[i], other[i + 1] = i + 1, i
+    pairs = [(i * ny + j, other[i] * ny + j if i in other else i * ny + (j ^ 1)) for i in range(nx) for j in range(ny)]
+    return lax.ppermute(x, ("gx", "gy"), pairs)
 
 
 def one_sample(k, s, p, q):
@@ -369,7 +384,7 @@
     from_prev, from_next = ring(last, "gy", 1), ring(first, "gy", -1)
     message = (2 * NZ + 2 * TILES, ROWS, LANES)
     packed, to_prev, to_next = call(pack_rows, ((4,) + cols, message, message), (k, s, p, q, first, last, from_prev, from_next))
-    prev, nxt = ring(to_next, "gx", 1), ring(to_prev, "gx", -1)
+    prev, nxt = trade(to_prev, 1), trade(to_next, 0)
     size = lax.axis_size("gx") * lax.axis_size("gy")
     field, strip = (NZ, SPAN, LANES), (TILES, SPAN, LANES)
     mid = call(

time: 46.3 us -> 44.8 us (0.968)
  waiting for transfers between devices: 6.69 us -> 8.24 us
  starting transfers between devices: 8.31 us -> 6.93 us
  blocking collectives: 25.9 us -> 24.7 us
    ppermute x4 -> x2, starting transfers between devices: 8.31 us -> 3.22 us  [ring(): return lax.ppermute(x, axis, [(i, (i + by) % n) for i in range(n)])]
    ppermute x0 -> x2, waiting for transfers between devices: none -> 3.99 us  [trade(): return lax.ppermute(x, ('gx', 'gy'), pairs)]
    ppermute x0 -> x2, starting transfers between devices: none -> 3.71 us  [trade(): return lax.ppermute(x, ('gx', 'gy'), pairs)]
    ppermute x4 -> x2, waiting for transfers between devices: 6.69 us -> 4.25 us  [ring(): return lax.ppermute(x, axis, [(i, (i + by) % n) for i in range(n)])]
    all_to_all x1, blocking collectives: 25.9 us -> 24.7 us  [one_sample(): sums = lax.all_to_all(mid[0], ('gx', 'gy'), 0, 0, tiled=True)]
  transfers between devices with their start and end apart: 4 -> 4, of which waited for: 3 -> 4; matrix products, arithmetic and copies ran while one was open for 0% -> 0% of each run, Pallas kernels for 0% -> 0%
where the time goes in v4:
time: 44.8 us; the launch traced here: 44.7 us
  blocking collectives  24.7 us (55%)
  waiting for transfers between devices  8.24 us (18%)
  starting transfers between devices  6.93 us (15%)
  Pallas kernels  4.13 us (9%)
  between operations  0.66 us (1%)
    all_to_all x1, blocking collectives, one_sample(): sums = lax.all_to_all(mid[0], ('gx', 'gy'), 0, 0, tiled=True)  24.7 us
    ppermute x2, waiting for transfers between devices, ring(): return lax.ppermute(x, axis, [(i, (i + by) % n) for i in range(n)])  4.25 us
    ppermute x2, waiting for transfers between devices, trade(): return lax.ppermute(x, ('gx', 'gy'), pairs)  3.99 us
    ppermute x2, starting transfers between devices, trade(): return lax.ppermute(x, ('gx', 'gy'), pairs)  3.71 us
    ppermute x2, starting transfers between devices, ring(): return lax.ppermute(x, axis, [(i, (i + by) % n) for i in range(n)])  3.22 us
    pallas_call x2, Pallas kernels, call(): pl.pallas_call(body, name=body.__name__, out_shape=tuple((pltpu.VMEM(s, F...  1.65 us
    pallas_call x1, Pallas kernels, one_sample(): pl.pallas_call(pack_columns, name='pack_columns', out_shape=tuple((pltpu....  1.28 us
    pallas_call x1, Pallas kernels, one_sample(): pl.pallas_call(finish, name='finish', out_shape=(jax.ShapeDtypeStruct(own...  1.2 us
  transfers between devices with their start and end apart: 4, of which 4 were waited for; matrix products, arithmetic and copies ran while one was open for 0% of the time, Pallas kernels for 0%

profile of v4, /device:TPU:1, one launch (start us, length us, event | category | flops | bytes accessed | tf_op | source)
XLA Modules:
  0.0 44.7 jit_solution(17302578114689720488)
XLA Ops:
  0.6 1.3 %pack_columns.1 = (f32[2,8,128]{2,1,0:T(8,128)S(1)}, f32[2,8,128]{2,1,0:T(8,128)S(1)}, f32[16,8,128]{2,1,0:T(8,128)S(1)}, f32[16,8,128]{2,1,0:T(8,128)S(1)}, f32...) custom-call(f32[16,8,128]{2,1,0:T(8,128)} %bitcast.11, f32[16,8,128]{2,1,0:T(8,128)} %bitcast.12, ...), custom_call_target="tpu_custom_call" | custom-call | tf_op jit(solution)/shard_map/pack_columns/pallas_call | solution.py:376
  1.9 3.2 %collective-permute-start.1 = (f32[2,8,128]{2,1,0:T(8,128)S(1)}, f32[2,8,128]{2,1,0:T(8,128)S(1)}, u32[]{:S(2)}, u32[]{:S(2)}) collective-permute-start(f32[2,8,128]{2,1,0:T(8,128)S(1)} %get-tuple-element.30.own_first), channel_id=1, source_target_pairs={{0,15},{1,0},{2,1},{3,2},{4,3},{5,4},{6,5},{7,6},{8,7},{9,8},{10,9... | collective-permute-start | bytes 24584 | tf_op jit(solution)/shard_map/ppermute | solution.py:360
  5.1 0.0 collective-permute-start
  5.1 1.1 %collective-permute-done.1.from_next = f32[2,8,128]{2,1,0:T(8,128)S(1)} collective-permute-done((f32[2,8,128]{2,1,0:T(8,128)S(1)}, f32[2,8,128]{2,1,0:T(8,128)S(1)}, u32[]{:S(2)}, u32[]{:S(2)}) %collective-permute-start.1) | collective-permute-done | bytes 8224 | tf_op jit(solution)/shard_map/ppermute | solution.py:360
  6.3 3.1 %collective-permute-done.from_prev = f32[2,8,128]{2,1,0:T(8,128)S(1)} collective-permute-done((f32[2,8,128]{2,1,0:T(8,128)S(1)}, f32[2,8,128]{2,1,0:T(8,128)S(1)}, u32[]{:S(2)}, u32[]{:S(2)}) %collective-permute-start) | collective-permute-done | bytes 8224 | tf_op jit(solution)/shard_map/ppermute | solution.py:360
  9.4 0.1 pack_rows.1
  9.5 3.7 %collective-permute-start.2 = (f32[36,8,128]{2,1,0:T(8,128)S(1)}, f32[36,8,128]{2,1,0:T(8,128)S(1)}, u32[]{:S(2)}, u32[]{:S(2)}) collective-permute-start(f32[36,8,128]{2,1,0:T(8,128)S(1)} %get-tuple-element.33), channel_id=1, source_target_pairs={{0,1},{1,0},{2,3},{3,2},{4,5},{5,4},{6,7},{7,6},{8,9},{9,8},{10,11... | collective-permute-start | bytes 442376 | tf_op jit(solution)/shard_map/ppermute | solution.py:369
  13.2 0.0 collective-permute-start.3
  13.2 1.0 %collective-permute-done.2.prev = f32[36,8,128]{2,1,0:T(8,128)S(1)} collective-permute-done((f32[36,8,128]{2,1,0:T(8,128)S(1)}, f32[36,8,128]{2,1,0:T(8,128)S(1)}, u32[]{:S(2)}, u32[]{:S(2)}) %collective-permute-start.2) | collective-permute-done | bytes 147488 | tf_op jit(solution)/shard_map/ppermute | solution.py:369
  14.2 3.0 %collective-permute-done.3.nxt = f32[36,8,128]{2,1,0:T(8,128)S(1)} collective-permute-done((f32[36,8,128]{2,1,0:T(8,128)S(1)}, f32[36,8,128]{2,1,0:T(8,128)S(1)}, u32[]{:S(2)}, u32[]{:S(2)}) %collective-permute-start.3) | collective-permute-done | bytes 147488 | tf_op jit(solution)/shard_map/ppermute | solution.py:369
  17.2 1.6 %middle.1 = (f32[256,128]{1,0:T(8,128)S(1)}, f32[16,16,128]{2,1,0:T(8,128)S(1)}, f32[16,16,128]{2,1,0:T(8,128)S(1)}, f32[16,16,128]{2,1,0:T(8,128)S(1)}, f32[16,...) custom-call(f32[16,8,128]{2,1,0:T(8,128)S(1)} %get-tuple-element.26., ...), custom_call_target="tpu_custom_call" | custom-call | tf_op jit(solution)/shard_map/middle/pallas_call | solution.py:348
  18.8 24.7 %all_to_all.11 = f32[256,1,128]{2,1,0:T(1,128)S(1)} all-to-all(f32[256,1,128]{2,1,0:T(1,128)S(1)} %bitcast.10), channel_id=1, replica_groups=mesh['gx'=16,'gy'=16] {'gx','gy'}, dimensions={0} | all-to-all | bytes 262144 | tf_op jit(solution)/shard_map/all_to_all | solution.py:396
  43.5 1.2 %finish.1 = (f32[16,8,128]{2,1,0:T(8,128)}, f32[16,8,128]{2,1,0:T(8,128)}) custom-call(f32[256,128]{1,0:T(8,128)S(1)} %bitcast.9, f32[16,8,128]{2,1,0:T(8,128)S(1)} %get-tuple-element.28.p.p_own, f32[16,16,128]{2,1,0:T(8,128)S(1)} %get-tuple-element.36.z0, f32[16,16,128]{2,1,0:T(8,128)S(1)} %get-tuple-element.37.v, f32[16,16,128]{2,1,0:T(8,128)S(1)} %get-tuple-element.38.s, ...), custom_call_target="tpu_custom_call" | custom-call | tf_op jit(solution)/shard_map/finish/pallas_call | solution.py:398
Async XLA Ops:
  1.9 4.4 %collective-permute-start.1 = (f32[2,8,128]{2,1,0:T(8,128)S(1)}, f32[2,8,128]{2,1,0:T(8,128)S(1)}, u32[]{:S(2)}, u32[]{:S(2)}) collective-permute-start(f32[2,8,128]{2,1,0:T(8,128)S(1)} %get-tuple-element.30.own_first), channel_id=1, source_target_pairs={{0,15},{1,0},{2,1},{3,2},{4,3},{5,4},{6,5},{7,6},{8,7},{9,8},{10,9... | collective-permute-start | bytes 24584 | tf_op jit(solution)/shard_map/ppermute | solution.py:360
  5.1 4.3 %collective-permute-start = (f32[2,8,128]{2,1,0:T(8,128)S(1)}, f32[2,8,128]{2,1,0:T(8,128)S(1)}, u32[]{:S(2)}, u32[]{:S(2)}) collective-permute-start(f32[2,8,128]{2,1,0:T(8,128)S(1)} %get-tuple-element.31.own_last), channel_id=1, source_target_pairs={{0,1},{1,2},{2,3},{3,4},{4,5},{5,6},{6,7},{7,8},{8,9},{9,10},{10,1... | collective-permute-start | bytes 24584 | tf_op jit(solution)/shard_map/ppermute | solution.py:360
  9.5 4.7 %collective-permute-start.2 = (f32[36,8,128]{2,1,0:T(8,128)S(1)}, f32[36,8,128]{2,1,0:T(8,128)S(1)}, u32[]{:S(2)}, u32[]{:S(2)}) collective-permute-start(f32[36,8,128]{2,1,0:T(8,128)S(1)} %get-tuple-element.33), channel_id=1, source_target_pairs={{0,1},{1,0},{2,3},{3,2},{4,5},{5,4},{6,7},{7,6},{8,9},{9,8},{10,11... | collective-permute-start | bytes 442376 | tf_op jit(solution)/shard_map/ppermute | solution.py:369
  13.2 4.0 %collective-permute-start.3 = (f32[36,8,128]{2,1,0:T(8,128)S(1)}, f32[36,8,128]{2,1,0:T(8,128)S(1)}, u32[]{:S(2)}, u32[]{:S(2)}) collective-permute-start(f32[36,8,128]{2,1,0:T(8,128)S(1)} %get-tuple-element.34), channel_id=1, source_target_pairs={{0,16},{1,17},{2,18},{3,19},{4,20},{5,21},{6,22},{7,23},{8,24},{9,... | collective-permute-start | bytes 442376 | tf_op jit(solution)/shard_map/ppermute | solution.py:369

commit v5 on v4

--- a/solution.py
+++ b/solution.py
@@ -4,6 +4,7 @@
 from jax.experimental import pallas as pl
 from jax.experimental.pallas import tpu as pltpu
 from jax.sharding import PartitionSpec as P
+
 
 storage_term = 0.5
 vertical_ratio = 0.1
@@ -86,18 +87,23 @@
         to_next[t] = last[t]
 
 
-def pack_rows(k, s, p, q, own_first, own_last, from_prev, from_next, packed, to_prev, to_next):
+def pair(at, a, b, to_far, to_near):
+    odd = lax.axis_index("gx") % 2 == 1
+    low = sublanes() < HALO
+    before = jnp.where(low, a, turn(b, HALO, 0))
+    after = jnp.where(low, turn(a, HALO, 0), b)
+    to_far[at] = jnp.where(odd, after, before)
+    to_near[at] = jnp.where(odd, before, after)
+
+
+def pack_body(k, s, p, q, to_far, to_near):
+    for z in range(NZ):
+        pair(z, k[z], s[z], to_far, to_near)
+        pair(NZ + z, p[z], q[z], to_far, to_near)
+
+
+def pack_strip(own_first, own_last, from_prev, from_next, packed, to_far, to_near):
     seg = lanes() % SEG // 4
-    low = sublanes() < HALO
-
-    even = lax.axis_index("gx") % 2 == 1
-
-    def pair(at, a, b):
-        before = jnp.where(low, a, turn(b, HALO, 0))
-        after = jnp.where(low, turn(a, HALO, 0), b)
-        to_prev[at] = jnp.where(even, after, before)
-        to_next[at] = jnp.where(even, before, after)
-
     for t in range(TILES):
         cols = []
         for i in range(4):
@@ -107,12 +113,8 @@
             x = jnp.where(seg == 3, turn(from_next[t], 12 - 4 * i, 1), x)
             packed[i, t] = x
             cols.append(x)
-        pair(2 * NZ + t, cols[0], cols[1])
-        pair(2 * NZ + TILES + t, cols[2], cols[3])
-
-    for z in range(NZ):
-        pair(z, k[z], s[z])
-        pair(NZ + z, p[z], q[z])
+        pair(t, cols[0], cols[1], to_far, to_near)
+        pair(TILES + t, cols[2], cols[3], to_far, to_near)
 
 
 def layer_next(x):
@@ -151,7 +153,7 @@
     return jnp.where(lanes((SPAN, LANES)) == 0, pltpu.roll(packed_face[z // PER], at, 1), col_prev(y))
 
 
-def middle(k_own, s_own, p_own, q_own, packed, prev, nxt,
+def middle(k_own, s_own, p_own, q_own, packed, far, near, far_strip, near_strip,
            sums, z0, v, s, q, fp, fz, fv, s_pack, q_pack, fp_pack, fz_pack, fv_pack,
            k, p, cx, cy, cz, inv, r, cy_pack):
     gx, gy = lax.axis_index("gx"), lax.axis_index("gy")
@@ -162,15 +164,15 @@
     seg8 = lanes() % SEG // 4
     inside_cols = jnp.where(seg8 == 0, jnp.where(gy == 0, 0.0, 1.0), jnp.where(seg8 == 3, jnp.where(gy == last_gy, 0.0, 1.0), 1.0))
 
-    even = gx % 2 == 1
-
-    def halo_rows(at):
-        below, above = jnp.where(even, prev[at], nxt[at]), jnp.where(even, nxt[at], prev[at])
+    odd = gx % 2 == 1
+
+    def halo_rows(at, far, near):
+        below, above = jnp.where(odd, far[at], near[at]), jnp.where(odd, near[at], far[at])
         return jnp.where(low, below, turn(above, HALO, 0)), jnp.where(low, turn(below, HALO, 0), above)
 
     def assemble(z, _):
-        ka, sa = halo_rows(z)
-        pa, qa = halo_rows(NZ + z)
+        ka, sa = halo_rows(z, far, near)
+        pa, qa = halo_rows(NZ + z, far, near)
         k[z, :ROWS], k[z, ROWS:] = k_own[z], ka * inside_rows
         s[z, :ROWS], s[z, ROWS:] = s_own[z], sa
         p[z, :ROWS], p[z, ROWS:] = p_own[z], pa
@@ -181,8 +183,8 @@
 
     kp, sp, pp, qp = [], [], [], []
     for t in range(TILES):
-        ka, sa = halo_rows(2 * NZ + t)
-        pa, qa = halo_rows(2 * NZ + TILES + t)
+        ka, sa = halo_rows(t, far_strip, near_strip)
+        pa, qa = halo_rows(TILES + t, far_strip, near_strip)
         kp.append(jnp.concatenate([packed[0, t] * inside_cols, ka * inside_rows * inside_cols], 0))
         sp.append(jnp.concatenate([packed[1, t], sa], 0))
         pp.append(jnp.concatenate([packed[2, t], pa], 0))
@@ -347,7 +349,6 @@
     args = [pltpu.with_memory_space_constraint(x, pltpu.VMEM) for x in args]
     return pl.pallas_call(
         body,
-        name=body.__name__,
         out_shape=tuple(pltpu.VMEM(s, F32) for s in outs),
         in_specs=[VMEM] * len(args),
         out_specs=tuple(VMEM for _ in outs),
@@ -381,16 +382,20 @@
         out_specs=(VMEM,) * 6,
         scratch_shapes=[pltpu.SemaphoreType.DMA((4,))],
     )(k, s, p, q)
-    from_prev, from_next = ring(last, "gy", 1), ring(first, "gy", -1)
-    message = (2 * NZ + 2 * TILES, ROWS, LANES)
-    packed, to_prev, to_next = call(pack_rows, ((4,) + cols, message, message), (k, s, p, q, first, last, from_prev, from_next))
-    prev, nxt = trade(to_prev, 1), trade(to_next, 0)
+    from_prev = ring(last, "gy", 1)
+    from_next = ring(first, "gy", -1)
+    body, strips = (2 * NZ, ROWS, LANES), (2 * TILES, ROWS, LANES)
+    to_far, to_near = call(pack_body, (body, body), (k, s, p, q))
+    far = trade(to_far, 1)
+    near = trade(to_near, 0)
+    packed, to_far, to_near = call(pack_strip, ((4,) + cols, strips, strips), (first, last, from_prev, from_next))
+    far_strip, near_strip = trade(to_far, 1), trade(to_near, 0)
     size = lax.axis_size("gx") * lax.axis_size("gy")
     field, strip = (NZ, SPAN, LANES), (TILES, SPAN, LANES)
     mid = call(
         middle,
         ((size, LANES),) + (field,) * 4 + ((3,) + field,) * 3 + (strip,) * 2 + ((3,) + strip,) * 3,
-        (k, s, p, q, packed, prev, nxt),
+        (k, s, p, q, packed, far, near, far_strip, near_strip),
         (field,) * 7 + (strip,),
     )
     sums = lax.all_to_all(mid[0], ("gx", "gy"), 0, 0, tiled=True)

time: 44.8 us -> 45.6 us (1.018)
  starting transfers between devices: 6.93 us -> 9.97 us
  waiting for transfers between devices: 8.24 us -> 6.47 us
  blocking collectives: 24.7 us -> 24.1 us
    ppermute x2 -> x4, starting transfers between devices: 3.71 us -> 7.21 us  [trade(): return lax.ppermute(x, ('gx', 'gy'), pairs)]
    ppermute x2 -> x4, waiting for transfers between devices: 3.99 us -> 2.59 us  [trade(): return lax.ppermute(x, ('gx', 'gy'), pairs)]
    all_to_all x1, blocking collectives: 24.7 us -> 24.1 us  [one_sample(): sums = lax.all_to_all(mid[0], ('gx', 'gy'), 0, 0, tiled=True)]
    pallas_call x2 -> x3, Pallas kernels: 1.65 us -> 1.7 us  [call(): pl.pallas_call(body, out_shape=tuple((pltpu.VMEM(s, F32) for s in outs)),...]
  transfers between devices with their start and end apart: 4 -> 6, of which waited for: 4 -> 4; matrix products, arithmetic and copies ran while one was open for 0% -> 0% of each run, Pallas kernels for 0% -> 0%
where the time goes in v5:
time: 45.6 us; the launch traced here: 45.4 us
  blocking collectives  24.1 us (53%)
  starting transfers between devices  9.97 us (22%)
  waiting for transfers between devices  6.47 us (14%)
  Pallas kernels  4.18 us (9%)
  between operations  0.67 us (1%)
    all_to_all x1, blocking collectives, one_sample(): sums = lax.all_to_all(mid[0], ('gx', 'gy'), 0, 0, tiled=True)  24.1 us
    ppermute x4, starting transfers between devices, trade(): return lax.ppermute(x, ('gx', 'gy'), pairs)  7.21 us
    ppermute x2, waiting for transfers between devices, ring(): return lax.ppermute(x, axis, [(i, (i + by) % n) for i in range(n)])  3.87 us
    ppermute x2, starting transfers between devices, ring(): return lax.ppermute(x, axis, [(i, (i + by) % n) for i in range(n)])  2.76 us
    ppermute x4, waiting for transfers between devices, trade(): return lax.ppermute(x, ('gx', 'gy'), pairs)  2.59 us
    pallas_call x3, Pallas kernels, call(): pl.pallas_call(body, out_shape=tuple((pltpu.VMEM(s, F32) for s in outs)),...  1.7 us
    pallas_call x1, Pallas kernels, one_sample(): pl.pallas_call(pack_columns, name='pack_columns', out_shape=tuple((pltpu....  1.28 us
    pallas_call x1, Pallas kernels, one_sample(): pl.pallas_call(finish, name='finish', out_shape=(jax.ShapeDtypeStruct(own...  1.2 us
  transfers between devices with their start and end apart: 6, of which 4 were waited for; matrix products, arithmetic and copies ran while one was open for 0% of the time, Pallas kernels for 0%

profile of v5, /device:TPU:1, one launch (start us, length us, event | category | flops | bytes accessed | tf_op | source)
XLA Modules:
  0.0 45.4 jit_solution(1805328229488891097)
XLA Ops:
  0.6 1.3 %pack_columns.1 = (f32[2,8,128]{2,1,0:T(8,128)S(1)}, f32[2,8,128]{2,1,0:T(8,128)S(1)}, f32[16,8,128]{2,1,0:T(8,128)S(1)}, f32[16,8,128]{2,1,0:T(8,128)S(1)}, f32...) custom-call(f32[16,8,128]{2,1,0:T(8,128)} %bitcast.11, f32[16,8,128]{2,1,0:T(8,128)} %bitcast.12, ...), custom_call_target="tpu_custom_call" | custom-call | tf_op jit(solution)/shard_map/pack_columns/pallas_call | solution.py:377
  2.0 3.3 %collective-permute-start.2 = (f32[32,8,128]{2,1,0:T(8,128)S(1)}, f32[32,8,128]{2,1,0:T(8,128)S(1)}, u32[]{:S(2)}, u32[]{:S(2)}) collective-permute-start(f32[32,8,128]{2,1,0:T(8,128)S(1)} %get-tuple-element.35), channel_id=1, source_target_pairs={{0,1},{1,0},{2,3},{3,2},{4,5},{5,4},{6,7},{7,6},{8,9},{9,8},{10,11... | collective-permute-start | bytes 393224 | tf_op jit(solution)/shard_map/ppermute | solution.py:370
  5.2 0.2 collective-permute-start.3
  5.5 1.2 %collective-permute-start.1 = (f32[2,8,128]{2,1,0:T(8,128)S(1)}, f32[2,8,128]{2,1,0:T(8,128)S(1)}, u32[]{:S(2)}, u32[]{:S(2)}) collective-permute-start(f32[2,8,128]{2,1,0:T(8,128)S(1)} %get-tuple-element.32.own_first), channel_id=1, source_target_pairs={{0,15},{1,0},{2,1},{3,2},{4,3},{5,4},{6,5},{7,6},{8,7},{9,8},{10,9... | collective-permute-start | bytes 24584 | tf_op jit(solution)/shard_map/ppermute | solution.py:361
  6.7 1.5 %collective-permute-start = (f32[2,8,128]{2,1,0:T(8,128)S(1)}, f32[2,8,128]{2,1,0:T(8,128)S(1)}, u32[]{:S(2)}, u32[]{:S(2)}) collective-permute-start(f32[2,8,128]{2,1,0:T(8,128)S(1)} %get-tuple-element.33.own_last), channel_id=1, source_target_pairs={{0,1},{1,2},{2,3},{3,4},{4,5},{5,6},{6,7},{7,8},{8,9},{9,10},{10,1... | collective-permute-start | bytes 24584 | tf_op jit(solution)/shard_map/ppermute | solution.py:361
  8.2 1.6 %collective-permute-done.1.from_next = f32[2,8,128]{2,1,0:T(8,128)S(1)} collective-permute-done((f32[2,8,128]{2,1,0:T(8,128)S(1)}, f32[2,8,128]{2,1,0:T(8,128)S(1)}, u32[]{:S(2)}, u32[]{:S(2)}) %collective-permute-start.1) | collective-permute-done | bytes 8224 | tf_op jit(solution)/shard_map/ppermute | solution.py:361
  9.8 2.2 %collective-permute-done.from_prev = f32[2,8,128]{2,1,0:T(8,128)S(1)} collective-permute-done((f32[2,8,128]{2,1,0:T(8,128)S(1)}, f32[2,8,128]{2,1,0:T(8,128)S(1)}, u32[]{:S(2)}, u32[]{:S(2)}) %collective-permute-start) | collective-permute-done | bytes 8224 | tf_op jit(solution)/shard_map/ppermute | solution.py:361
  12.1 0.1 shard_map.59
  12.2 3.7 %collective-permute-start.4 = (f32[4,8,128]{2,1,0:T(8,128)S(1)}, f32[4,8,128]{2,1,0:T(8,128)S(1)}, u32[]{:S(2)}, u32[]{:S(2)}) collective-permute-start(f32[4,8,128]{2,1,0:T(8,128)S(1)} %get-tuple-element.37), channel_id=1, source_target_pairs={{0,1},{1,0},{2,3},{3,2},{4,5},{5,4},{6,7},{7,6},{8,9},{9,8},{10,11... | collective-permute-start | bytes 49160 | tf_op jit(solution)/shard_map/ppermute | solution.py:370
  15.9 0.0 collective-permute-start.5
  15.9 0.8 %collective-permute-done.4.far_strip = f32[4,8,128]{2,1,0:T(8,128)S(1)} collective-permute-done((f32[4,8,128]{2,1,0:T(8,128)S(1)}, f32[4,8,128]{2,1,0:T(8,128)S(1)}, u32[]{:S(2)}, u32[]{:S(2)}) %collective-permute-start.4) | collective-permute-done | bytes 16416 | tf_op jit(solution)/shard_map/ppermute | solution.py:370
  16.7 1.8 %collective-permute-done.5.near_strip = f32[4,8,128]{2,1,0:T(8,128)S(1)} collective-permute-done((f32[4,8,128]{2,1,0:T(8,128)S(1)}, f32[4,8,128]{2,1,0:T(8,128)S(1)}, u32[]{:S(2)}, u32[]{:S(2)}) %collective-permute-start.5) | collective-permute-done | bytes 16416 | tf_op jit(solution)/shard_map/ppermute | solution.py:370
  18.5 0.0 collective-permute-done.2.far
  18.5 0.0 collective-permute-done.3.near
  18.5 1.6 %shard_map.61 = (f32[256,128]{1,0:T(8,128)S(1)}, f32[16,16,128]{2,1,0:T(8,128)S(1)}, f32[16,16,128]{2,1,0:T(8,128)S(1)}, f32[16,16,128]{2,1,0:T(8,128)S(1)}, f32...) custom-call(f32[16,8,128]{2,1,0:T(8,128)S(1)} %get-tuple-element.28., ...), custom_call_target="tpu_custom_call" | custom-call | tf_op jit(solution)/shard_map/pallas_call | solution.py:350
  20.1 24.1 %all_to_all.11 = f32[256,1,128]{2,1,0:T(1,128)S(1)} all-to-all(f32[256,1,128]{2,1,0:T(1,128)S(1)} %bitcast.10), channel_id=1, replica_groups=mesh['gx'=16,'gy'=16] {'gx','gy'}, dimensions={0} | all-to-all | bytes 262144 | tf_op jit(solution)/shard_map/all_to_all | solution.py:401
  44.2 1.2 %finish.1 = (f32[16,8,128]{2,1,0:T(8,128)}, f32[16,8,128]{2,1,0:T(8,128)}) custom-call(f32[256,128]{1,0:T(8,128)S(1)} %bitcast.9, f32[16,8,128]{2,1,0:T(8,128)S(1)} %get-tuple-element.30.p.p_own, f32[16,16,128]{2,1,0:T(8,128)S(1)} %get-tuple-element.40.z0, f32[16,16,128]{2,1,0:T(8,128)S(1)} %get-tuple-element.41.v, f32[16,16,128]{2,1,0:T(8,128)S(1)} %get-tuple-element.42.s, ...), custom_call_target="tpu_custom_call" | custom-call | tf_op jit(solution)/shard_map/finish/pallas_call | solution.py:403
  (1 shorter events, 0.0 us)
Async XLA Ops:
  2.0 16.5 %collective-permute-start.2 = (f32[32,8,128]{2,1,0:T(8,128)S(1)}, f32[32,8,128]{2,1,0:T(8,128)S(1)}, u32[]{:S(2)}, u32[]{:S(2)}) collective-permute-start(f32[32,8,128]{2,1,0:T(8,128)S(1)} %get-tuple-element.35), channel_id=1, source_target_pairs={{0,1},{1,0},{2,3},{3,2},{4,5},{5,4},{6,7},{7,6},{8,9},{9,8},{10,11... | collective-permute-start | bytes 393224 | tf_op jit(solution)/shard_map/ppermute | solution.py:370
  5.2 13.3 %collective-permute-start.3 = (f32[32,8,128]{2,1,0:T(8,128)S(1)}, f32[32,8,128]{2,1,0:T(8,128)S(1)}, u32[]{:S(2)}, u32[]{:S(2)}) collective-permute-start(f32[32,8,128]{2,1,0:T(8,128)S(1)} %get-tuple-element.36), channel_id=1, source_target_pairs={{0,16},{1,17},{2,18},{3,19},{4,20},{5,21},{6,22},{7,23},{8,24},{9,... | collective-permute-start | bytes 393224 | tf_op jit(solution)/shard_map/ppermute | solution.py:370
  5.5 4.4 %collective-permute-start.1 = (f32[2,8,128]{2,1,0:T(8,128)S(1)}, f32[2,8,128]{2,1,0:T(8,128)S(1)}, u32[]{:S(2)}, u32[]{:S(2)}) collective-permute-start(f32[2,8,128]{2,1,0:T(8,128)S(1)} %get-tuple-element.32.own_first), channel_id=1, source_target_pairs={{0,15},{1,0},{2,1},{3,2},{4,3},{5,4},{6,5},{7,6},{8,7},{9,8},{10,9... | collective-permute-start | bytes 24584 | tf_op jit(solution)/shard_map/ppermute | solution.py:361
  6.7 5.4 %collective-permute-start = (f32[2,8,128]{2,1,0:T(8,128)S(1)}, f32[2,8,128]{2,1,0:T(8,128)S(1)}, u32[]{:S(2)}, u32[]{:S(2)}) collective-permute-start(f32[2,8,128]{2,1,0:T(8,128)S(1)} %get-tuple-element.33.own_last), channel_id=1, source_target_pairs={{0,1},{1,2},{2,3},{3,4},{4,5},{5,6},{6,7},{7,8},{8,9},{9,10},{10,1... | collective-permute-start | bytes 24584 | tf_op jit(solution)/shard_map/ppermute | solution.py:361
  12.2 4.5 %collective-permute-start.4 = (f32[4,8,128]{2,1,0:T(8,128)S(1)}, f32[4,8,128]{2,1,0:T(8,128)S(1)}, u32[]{:S(2)}, u32[]{:S(2)}) collective-permute-start(f32[4,8,128]{2,1,0:T(8,128)S(1)} %get-tuple-element.37), channel_id=1, source_target_pairs={{0,1},{1,0},{2,3},{3,2},{4,5},{5,4},{6,7},{7,6},{8,9},{9,8},{10,11... | collective-permute-start | bytes 49160 | tf_op jit(solution)/shard_map/ppermute | solution.py:370
  15.9 2.6 %collective-permute-start.5 = (f32[4,8,128]{2,1,0:T(8,128)S(1)}, f32[4,8,128]{2,1,0:T(8,128)S(1)}, u32[]{:S(2)}, u32[]{:S(2)}) collective-permute-start(f32[4,8,128]{2,1,0:T(8,128)S(1)} %get-tuple-element.38), channel_id=1, source_target_pairs={{0,16},{1,17},{2,18},{3,19},{4,20},{5,21},{6,22},{7,23},{8,24},{9,... | collective-permute-start | bytes 49160 | tf_op jit(solution)/shard_map/ppermute | solution.py:370
